TPU v7x, 512 devices: a whole 4x4x16 slice. The times are simulated.
512 devices in a mesh: tile: 128 (over y, z_hi, x, core), grp: 4 (over z_lo).
Axes of the slice: x: 4, y: 4, z: 16 (z_hi: 4, z_lo: 4; z = z_hi * 4 + z_lo), core: 2. Of those that a mesh axis runs over, the one named last changes fastest.
Arguments:
- forcing_vector: float32 [70, 1024, 512], P(None, 'tile', 'grp'), may hold values from -8 to 8
- shift_weights: float32 [70, 1024, 512], P(None, 'tile', 'grp'), may hold values from 0.0001 to 0.0004
- layer_link_factor: float32 [69], replicated, may hold values from 0.5 to 8
- previous_kelvin_field: float32 [70, 8, 65536], P(None, None, ('tile', 'grp')), may hold values from 0.8 to 1.2
- longwave_opacity: float32 [70], replicated, may hold values from 0.02 to 0.5
- shortwave_opacity: float32 [70], replicated, may hold values from 0.01 to 0.05
Outputs:
- solution_field: float32 [70, 1024, 512], P(None, 'tile', 'grp')
- radiation_state: float32 [70, 8, 65536], P(None, None, ('tile', 'grp'))
All inputs are finite; a program needn't handle non-finite values.
Results may differ from a plain program's by a relative error of at most 0.0003.
Values sent between devices are 32-bit elements; how exact they have to be, the bound alone decides.
A program may use at most 64 MiB of HBM per device.

v0:
```python
import math

import jax
import jax.numpy as jnp
from jax import lax
from jax.sharding import Mesh
from jax.sharding import PartitionSpec as P

LAYER_TOTAL = 70
SHARD_POINTS = 8
CY = 128
ITERS = 2
TILE_GRP = ("tile_0", "tile_1", "tile_2", "tile_3", "grp")
TILE = ("tile_0", "tile_1", "tile_2", "tile_3")


def padded_2(value, sides, width):
    edges = {}
    for axis, dim in sides:
        devices, length = (lax.axis_size(axis), value.shape[dim])
        up = [(i, (i + 1) % devices) for i in range(devices)]
        last = lax.slice_in_dim(value, length - width, length, axis=dim)
        first = lax.slice_in_dim(value, 0, width, axis=dim)
        edges[dim] = (
            lax.ppermute(last, axis, up),
            lax.ppermute(first, axis, [(b, a) for a, b in up]),
        )
    done = []
    for _, dim in sides:
        low, high = edges[dim]
        around = [(width, width) if d in done else (0, 0) for d in range(value.ndim)]
        value = jnp.concatenate([jnp.pad(low, around), value, jnp.pad(high, around)], axis=dim)
        done.append(dim)
    return value


def in_order(parts, dim):
    parts = jnp.moveaxis(parts, 0, dim)
    dims = parts.shape
    return parts.reshape(*dims[:dim], dims[dim] * dims[dim + 1], *dims[dim + 2 :])


def gather_together(arrays, axis, dims):
    vector = jnp.concatenate([a.reshape(-1) for a in arrays])
    lines, at, gathered = (lax.all_gather(vector, axis), 0, [])
    for a, dim in zip(arrays, dims):
        parts = lines[:, at : at + a.size].reshape(-1, *a.shape)
        gathered.append(in_order(parts, dim))
        at += a.size
    return tuple(gathered)


def over_axes(value, axes):
    for axis in axes:
        value = lax.psum(value, axis)
    return value


def in_blocks(value, dim, devices):
    dims = value.shape
    parts = value.reshape(*dims[:dim], devices, dims[dim] // devices, *dims[dim + 1 :])
    return jnp.moveaxis(parts, dim, 0)


def exchange_in_order(parts, axes, turns):
    inside = parts.shape[1:]
    result = parts.reshape(*(lax.axis_size(a) for a in axes), *inside)
    for k in turns:
        result = lax.all_to_all(result, axes[k], k, k, tiled=True)
    return result.reshape(-1, *inside)


def core_and_chips(value, groups, turns, split_dim, concat_dim):
    devices = lax.axis_size(groups[0]) * lax.axis_size(groups[1])
    parts = in_blocks(value, split_dim, devices)
    return in_order(exchange_in_order(parts, groups, turns), concat_dim)


def column_inverse(layer_link_factor):
    size = layer_link_factor.shape[0] + 1
    zero_one = jnp.zeros((1,), jnp.float32)
    upper = jnp.concatenate([layer_link_factor, zero_one])
    lower = jnp.concatenate([zero_one, layer_link_factor])
    matrix = (
        jnp.diag(4.0 + upper + lower)
        - jnp.diag(layer_link_factor, 1)
        - jnp.diag(layer_link_factor, -1)
    )
    factor = jnp.linalg.cholesky(matrix)
    return jax.scipy.linalg.cho_solve((factor, True), jnp.eye(size, dtype=jnp.float32))


def radiation_tables(longwave_opacity, shortwave_opacity):
    levels = longwave_opacity.shape[0]
    transmitted = jnp.exp(-longwave_opacity)
    zero_one = jnp.zeros((1,), jnp.float32)
    interfaces = jnp.concatenate([zero_one, jnp.cumsum(longwave_opacity)])
    interface_index = jnp.arange(levels + 1)[:, None]
    layer_index = jnp.arange(levels)[None, :]
    below_mask = layer_index < interface_index
    gap_down = jnp.where(below_mask, interfaces[:, None] - interfaces[None, 1:], 0.0)
    downward = jnp.where(below_mask, jnp.exp(-gap_down), 0.0) * (1.0 - transmitted)[None, :]
    above_mask = layer_index >= interface_index
    gap_up = jnp.where(above_mask, interfaces[None, :-1] - interfaces[:, None], 0.0)
    upward = jnp.where(above_mask, jnp.exp(-gap_up), 0.0) * (1.0 - transmitted)[None, :]
    surface = jnp.exp(-(interfaces[-1] - interfaces))
    upward = upward.at[:, levels - 1].add(surface)
    matrix = downward[:-1] - downward[1:] + upward[1:] - upward[:-1]
    solar_edges = jnp.concatenate([zero_one, jnp.cumsum(shortwave_opacity)])
    absorbed = 10.0 * (jnp.exp(-solar_edges[:-1]) - jnp.exp(-solar_edges[1:]))
    return (matrix, absorbed)


def sun_cosine(global_row, total_rows):
    latitude = ((global_row.astype(jnp.float32) + 0.5) / total_rows - 0.5) * (math.pi / 2)
    return jnp.cos(latitude - 0.4)


def vertical(source, layer_link_factor):
    fluxes = layer_link_factor[:, None, None] * (source[:-1] - source[1:])
    zeros_level = jnp.zeros_like(source[:1])
    return jnp.concatenate([fluxes, zeros_level], axis=0) - jnp.concatenate(
        [zeros_level, fluxes], axis=0
    )


def operate(source, shift_weights, layer_link_factor, group_index, group_count):
    padded = padded_2(source, ((TILE, 1), ("grp", 2)), 1)
    lower_rim = jnp.where(group_index > 0, padded[:, 1:-1, 0:1], source[:, :, 0:1])
    upper_rim = jnp.where(group_index < group_count - 1, padded[:, 1:-1, -1:], source[:, :, -1:])
    across = jnp.concatenate([lower_rim, source[:, :, :-1]], axis=2) + jnp.concatenate(
        [source[:, :, 1:], upper_rim], axis=2
    )
    beside = padded[:, 2:, 1:-1] + padded[:, :-2, 1:-1] + across
    return shift_weights * source + 4.0 * source - beside + vertical(source, layer_link_factor)


def coarse_matrix(block_mass, tile_count, group_count):
    block_count = tile_count * group_count
    ordering = jnp.arange(block_count)
    tile_of = ordering // group_count
    group_of = ordering % group_count
    same_group = group_of[:, None] == group_of[None, :]
    tile_gap = (tile_of[:, None] - tile_of[None, :]) % tile_count
    x_near = same_group & ((tile_gap == 1) | (tile_gap == tile_count - 1))
    same_tile = tile_of[:, None] == tile_of[None, :]
    y_near = (same_tile & (jnp.abs(group_of[:, None] - group_of[None, :]) == 1)).astype(jnp.float32)
    y_count = jnp.sum(y_near, axis=1)
    diagonal = block_mass + 2.0 * LAYER_TOTAL * CY + LAYER_TOTAL * SHARD_POINTS * y_count
    return (
        jnp.diag(diagonal)
        - LAYER_TOTAL * CY * x_near.astype(jnp.float32)
        - LAYER_TOTAL * SHARD_POINTS * y_near
    )


def element(vector, position):
    return lax.dynamic_index_in_dim(vector, position, 0, keepdims=False)


def orthogonalize(direction, operator_image, weights, directions, images):
    direction = direction - weights[0] * directions[0]
    operator_image = operator_image - weights[0] * images[0]
    return (direction, operator_image)


def per_device(
    forcing_vector,
    shift_weights,
    layer_link_factor,
    previous_kelvin_field,
    longwave_opacity,
    shortwave_opacity,
):
    highest = lax.Precision.HIGHEST
    tile_count = lax.axis_size(TILE)
    group_count = lax.axis_size("grp")
    tile_index = lax.axis_index(TILE)
    group_index = lax.axis_index("grp")
    matrix, absorbed = radiation_tables(longwave_opacity, shortwave_opacity)
    share_rows = CY // tile_count
    position = jnp.arange(CY)
    global_row = group_index * CY + tile_index * share_rows + position % share_rows
    cosine = sun_cosine(global_row, CY * group_count)
    second_power_entry = previous_kelvin_field * previous_kelvin_field
    emission = second_power_entry * second_power_entry
    column_heating = jnp.dot(matrix, emission.reshape(LAYER_TOTAL, -1), precision=highest).reshape(
        emission.shape
    )
    column_heating = column_heating + absorbed[:, None, None] * cosine[None, None, :]
    column_heating = column_heating - jnp.mean(column_heating, axis=0, keepdims=True)
    heating = lax.all_to_all(column_heating, TILE, split_axis=2, concat_axis=2, tiled=True)
    forcing = forcing_vector + heating
    inverse = column_inverse(layer_link_factor)
    own_index = tile_index * group_count + group_index
    block_mass = jnp.sum(shift_weights).reshape(1)
    x_index = jnp.arange(SHARD_POINTS)[:, None]
    y_index = jnp.arange(CY)[None, :]
    factor = None
    solution = jnp.zeros_like(forcing)
    residual = forcing
    directions = []
    images = []
    image_norms = []
    gram_matrix = None
    residual_products = None
    for number in range(ITERS):
        smooth = jnp.dot(inverse, residual.reshape(LAYER_TOTAL, -1), precision=highest).reshape(
            residual.shape
        )
        smooth_image = operate(smooth, shift_weights, layer_link_factor, group_index, group_count)
        remainder = residual - smooth_image
        mass_all, sums_all = gather_together(
            (block_mass, jnp.sum(remainder).reshape(1)), TILE_GRP, (0, 0)
        )
        if factor is None:
            factor = jnp.linalg.cholesky(coarse_matrix(mass_all, tile_count, group_count))
        coarse = jax.scipy.linalg.cho_solve((factor, True), sums_all)
        own_value = element(coarse, own_index)
        direction = smooth + own_value
        coarse_west = element(coarse, (tile_index - 1) % tile_count * group_count + group_index)
        coarse_east = element(coarse, (tile_index + 1) % tile_count * group_count + group_index)
        coarse_south = element(coarse, jnp.maximum(own_index - 1, 0))
        coarse_north = element(coarse, jnp.minimum(own_index + 1, tile_count * group_count - 1))
        south_live = (group_index > 0).astype(jnp.float32)
        north_live = (group_index < group_count - 1).astype(jnp.float32)
        rim_terms = (x_index == 0).astype(jnp.float32) * (own_value - coarse_west)
        rim_terms = rim_terms + (x_index == SHARD_POINTS - 1).astype(jnp.float32) * (
            own_value - coarse_east
        )
        rim_terms = rim_terms + (y_index == 0).astype(jnp.float32) * south_live * (
            own_value - coarse_south
        )
        rim_terms = rim_terms + (y_index == CY - 1).astype(jnp.float32) * north_live * (
            own_value - coarse_north
        )
        operator_image = smooth_image + shift_weights * own_value + rim_terms[None]
        partial_value = jnp.stack(
            [jnp.sum(operator_image * earlier) for earlier in images]
            + [jnp.sum(residual * operator_image), jnp.sum(operator_image * operator_image)]
        )
        totals = over_axes(partial_value, TILE_GRP)
        crossing = totals[:number]
        projection = totals[number]
        image_norm = totals[number + 1]
        if number > 0:
            weights = crossing / jnp.diagonal(gram_matrix)
            new_row = crossing - jnp.dot(gram_matrix, weights, precision=highest)
            image_norm = (
                image_norm
                - 2.0 * jnp.sum(weights * crossing)
                + jnp.dot(
                    weights, jnp.dot(gram_matrix, weights, precision=highest), precision=highest
                )
            )
            projection = projection - jnp.sum(weights * residual_products)
            direction, operator_image = orthogonalize(
                direction, operator_image, weights, directions, images
            )
        step_size = projection / image_norm
        if number == 0:
            gram_matrix = image_norm.reshape(1, 1)
            residual_products = (projection - step_size * image_norm).reshape(1)
        else:
            upper_block = jnp.concatenate([gram_matrix, new_row[:, None]], axis=1)
            lower_block = jnp.concatenate([new_row, image_norm.reshape(1)])[None, :]
            gram_matrix = jnp.concatenate([upper_block, lower_block], axis=0)
            residual_products = jnp.concatenate(
                [
                    residual_products - step_size * new_row,
                    (projection - step_size * image_norm).reshape(1),
                ]
            )
        solution = solution + step_size * direction
        residual = residual - step_size * operator_image
        directions.append(direction)
        images.append(operator_image)
        image_norms.append(image_norm)
    radiation_state = core_and_chips(
        solution, (("tile_0", "tile_1", "tile_2"), "tile_3"), (0, 1), 2, 2
    )
    return (solution, radiation_state)


def solution(mesh):
    finer = Mesh(
        mesh.devices.reshape(4, 4, 4, 2, mesh.shape["grp"]),
        ("tile_0", "tile_1", "tile_2", "tile_3", "grp"),
    )
    placed = (P(None, TILE, "grp"), P(None, TILE, "grp"), P(), P(None, None, TILE_GRP), P(), P())
    return jax.shard_map(
        per_device,
        mesh=finer,
        in_specs=placed,
        out_specs=(P(None, TILE, "grp"), P(None, None, TILE_GRP)),
        check_vma=False,
    )
```

profile of v0, /device:TPU:1, one launch (start us, length us, event | category | flops | bytes accessed | tf_op | source)
XLA Modules:
  0.0 630.7 jit_solution(13307084892582990710)
XLA Ops:
  6.6 23.0 %all-to-all-start = ((f32[70,8,128]{0,1,2:T(8,128)}), f32[70,8,128]{0,1,2:T(8,128)S(1)}, u32[]{:S(2)}, u32[]{:S(2)}) async-start(f32[70,8,128]{0,1,2:T(8,128)} %copy.55), calls=%async_computation | async-start | bytes 1048576 | tf_op jit(solution)/shard_map/all_to_all | solution.py:192
  44.9 15.9 %all-to-all-done = f32[70,8,128]{0,1,2:T(8,128)S(1)} async-done(((f32[70,8,128]{0,1,2:T(8,128)}), f32[70,8,128]{0,1,2:T(8,128)S(1)}, u32[]{:S(2)}, u32[]{:S(2)}) %all-to-all-start) | async-done | bytes 286752 | tf_op jit(solution)/shard_map/all_to_all | solution.py:192
  62.0 8.1 %collective-permute-start.2 = (f32[70,8,1]{2,1,0:T(8,128)S(1)}, f32[70,8,1]{2,1,0:T(8,128)S(1)}, u32[]{:S(2)}, u32[]{:S(2)}) collective-permute-start(f32[70,8,1]{2,1,0:T(8,128)S(1)} %get-tuple-element.67), channel_id=1, source_target_pairs={{0,1},{1,2},{2,3},{3,0},{4,5},{5,6},{6,7},{7,4},{8,9},{9,10},{10,1... | collective-permute-start | bytes 6728 | tf_op jit(solution)/shard_map/ppermute | solution.py:25
  84.4 105.5 %all-reduce.7 = f32[1024]{0:T(1024)S(1)} all-reduce(f32[1024]{0:T(1024)S(1)} %maximum_dynamic-update-slice_fusion), channel_id=2, replica_groups=mesh['tile_0'=4,'tile_1'=4,'tile_2'=4,'tile_3'=2,'grp'=4] {'tile_0','til..., use_global_device_ids=true, to_apply=%add.7 | all-reduce | flops 1024 | bytes 8192
  192.4 11.7 %cholesky.130 = f32[128,128]{1,0:T(8,128)S(1)} custom-call(f32[128,128]{1,0:T(8,128)S(1)} %cholesky.299), custom_call_target="Cholesky" | custom-call | tf_op jit(solution)/shard_map/jit(cholesky)/cholesky | solution.py:217
  204.3 9.8 %custom-call.43 = f32[1,128,128]{1,2,0:T(8,128)S(1)} custom-call(f32[1,128,128]{2,1,0:T(8,128)S(1)} %get-tuple-element.85), custom_call_target="InvertDiagBlocksLowerTriangular" | custom-call | tf_op jit(solution)/shard_map/jit(cholesky)/cholesky | solution.py:217
  214.8 12.7 %cholesky.251 = f32[128,128]{1,0:T(8,128)} custom-call(f32[128,128]{1,0:T(8,128)S(1)} %cholesky.303), custom_call_target="Cholesky" | custom-call | tf_op jit(solution)/shard_map/jit(cholesky)/cholesky | solution.py:217
  229.7 10.4 %custom-call.44 = f32[1,128,128]{1,2,0:T(8,128)} custom-call(f32[1,128,128]{2,1,0:T(8,128)S(1)} %get-tuple-element.82), custom_call_target="InvertDiagBlocksLowerTriangular" | custom-call | tf_op jit(solution)/shard_map/jit(cholesky)/cholesky | solution.py:217
  241.6 11.7 %cholesky.272 = f32[128,128]{1,0:T(8,128)S(1)} custom-call(f32[128,128]{1,0:T(8,128)S(1)} %cholesky.308), custom_call_target="Cholesky" | custom-call | tf_op jit(solution)/shard_map/jit(cholesky)/cholesky | solution.py:217
  254.1 9.8 %custom-call.45 = f32[1,128,128]{1,2,0:T(8,128)S(1)} custom-call(f32[1,128,128]{2,1,0:T(8,128)S(1)} %get-tuple-element.79), custom_call_target="InvertDiagBlocksLowerTriangular" | custom-call | tf_op jit(solution)/shard_map/jit(cholesky)/cholesky | solution.py:217
  264.5 11.9 %cholesky.289 = f32[128,128]{1,0:T(8,128)S(1)} custom-call(f32[128,128]{1,0:T(8,128)S(1)} %convolution_subtract_fusion.2), custom_call_target="Cholesky" | custom-call | tf_op jit(solution)/shard_map/jit(cholesky)/cholesky | solution.py:217
  279.6 10.6 %while.5 = (s32[]{:T(128)}, f32[512,512]{1,0:T(8,128)S(1)}, s32[4,2]{0,1:T(2,128)S(1)}, f32[4,128,128]{2,1,0:T(8,128)}, s32[]{:T(128)}) while((s32[]{:T(128)}, f32[512,512]{1,0:T(8,128)S(1)}, s32[4,2]{0,1:T(2,128)S(1)}, f32[4,128,128]{2,1,0:T(8,128)}, s32[]{:T(128)}) %tuple.76), condition=%wide.while_cond.1, body=%wide.while_body.1.sunk | while | flops 2 | bytes 132705 | solution.py:218
  290.2 40.1 %custom-call.47 = f32[4,128,128]{1,2,0:T(8,128)S(1)} custom-call(f32[4,128,128]{2,1,0:T(8,128)} %get-tuple-element.29), custom_call_target="InvertDiagBlocksLowerTriangular" | custom-call | tf_op jit(solution)/shard_map/jit(_cho_solve)/triangular_solve | solution.py:218
  341.7 8.5 %psum.70 = f32[2]{0:T(128)S(1)} all-reduce(f32[2]{0:T(128)S(1)} %pad_maximum_fusion.8), channel_id=1, replica_groups=mesh['tile_0'=4,'tile_1'=4,'tile_2'=4,'tile_3'=2,'grp'=4] {'tile_0'}, use_global_device_ids=true, to_apply=%region_18.20 | all-reduce | flops 2 | bytes 16 | tf_op jit(solution)/shard_map/psum | solution.py:55
  350.2 11.3 %psum.71 = f32[2]{0:T(128)S(1)} all-reduce(f32[2]{0:T(128)S(1)} %psum.70), channel_id=1, replica_groups=mesh['tile_0'=4,'tile_1'=4,'tile_2'=4,'tile_3'=2,'grp'=4] {'tile_1'}, use_global_device_ids=true, to_apply=%region_19.21 | all-reduce | flops 2 | bytes 16 | tf_op jit(solution)/shard_map/psum | solution.py:55
  367.6 8.6 %psum.73 = f32[2]{0:T(128)S(1)} all-reduce(f32[2]{0:T(128)S(1)} %psum.72), channel_id=1, replica_groups=mesh['tile_0'=4,'tile_1'=4,'tile_2'=4,'tile_3'=2,'grp'=4] {'tile_3'}, use_global_device_ids=true, to_apply=%region_21.23 | all-reduce | flops 2 | bytes 16 | tf_op jit(solution)/shard_map/psum | solution.py:55
  376.1 8.7 %psum.74 = f32[2]{0:T(128)S(1)} all-reduce(f32[2]{0:T(128)S(1)} %psum.73), channel_id=1, replica_groups=mesh['tile_0'=4,'tile_1'=4,'tile_2'=4,'tile_3'=2,'grp'=4] {'grp'}, use_global_device_ids=true, to_apply=%region_22.24 | all-reduce | flops 2 | bytes 16 | tf_op jit(solution)/shard_map/psum | solution.py:55
  411.5 104.1 %all-reduce.8 = f32[1024]{0:T(1024)S(1)} all-reduce(f32[1024]{0:T(1024)S(1)} %maximum_dynamic-update-slice_fusion.1), channel_id=3, replica_groups=mesh['tile_0'=4,'tile_1'=4,'tile_2'=4,'tile_3'=2,'grp'=4] {'tile_0','til..., use_global_device_ids=true, to_apply=%add.8 | all-reduce | flops 1024 | bytes 8192
  538.6 11.2 %psum.76 = f32[3]{0:T(128)S(1)} all-reduce(f32[3]{0:T(128)S(1)} %psum.75), channel_id=1, replica_groups=mesh['tile_0'=4,'tile_1'=4,'tile_2'=4,'tile_3'=2,'grp'=4] {'tile_1'}, use_global_device_ids=true, to_apply=%region_28.30 | all-reduce | flops 3 | bytes 24 | tf_op jit(solution)/shard_map/psum | solution.py:55
  556.5 8.6 %psum.78 = f32[3]{0:T(128)S(1)} all-reduce(f32[3]{0:T(128)S(1)} %psum.77), channel_id=1, replica_groups=mesh['tile_0'=4,'tile_1'=4,'tile_2'=4,'tile_3'=2,'grp'=4] {'tile_3'}, use_global_device_ids=true, to_apply=%region_30.32 | all-reduce | flops 3 | bytes 24 | tf_op jit(solution)/shard_map/psum | solution.py:55
  565.6 9.0 %psum.79 = f32[3]{0:T(128)S(1)} all-reduce(f32[3]{0:T(128)S(1)} %psum.78), channel_id=1, replica_groups=mesh['tile_0'=4,'tile_1'=4,'tile_2'=4,'tile_3'=2,'grp'=4] {'grp'}, use_global_device_ids=true, to_apply=%region_31.33 | all-reduce | flops 3 | bytes 24 | tf_op jit(solution)/shard_map/psum | solution.py:55
  581.6 9.0 %all-to-all-start.1 = ((f32[64,2,70,8,1]{2,3,1,4,0:T(8,128)}), f32[64,2,70,8,1]{2,3,1,4,0:T(8,128)S(1)}, u32[]{:S(2)}, u32[]{:S(2)}) async-start(f32[64,2,70,8,1]{2,3,1,4,0:T(8,128)} %bitcast.116), calls=%async_computation.1 | async-start | bytes 1048576 | tf_op jit(solution)/shard_map/all_to_all | solution.py:69
  592.7 28.8 %all-to-all-done.1 = f32[64,2,70,8,1]{2,3,1,4,0:T(8,128)S(1)} async-done(((f32[64,2,70,8,1]{2,3,1,4,0:T(8,128)}), f32[64,2,70,8,1]{2,3,1,4,0:T(8,128)S(1)}, u32[]{:S(2)}, u32[]{:S(2)}) %all-to-all-start.1) | async-done | bytes 286752 | tf_op jit(solution)/shard_map/all_to_all | solution.py:69
  621.6 8.0 %all_to_all.15 = f32[64,2,70,8,1]{2,3,0,4,1:T(8,128)S(1)} all-to-all(f32[64,2,70,8,1]{2,3,0,4,1:T(8,128)S(1)} %copy.60), channel_id=1, replica_groups=mesh['tile_0'=4,'tile_1'=4,'tile_2'=4,'tile_3'=2,'grp'=4] {'tile_3'}, dimensions={1} | all-to-all | bytes 573440 | tf_op jit(solution)/shard_map/all_to_all | solution.py:69
  (194 shorter events, 123.4 us)
Async XLA Ops:
  0.6 3.4 copy-start.4
  6.6 54.2 %all-to-all-start = ((f32[70,8,128]{0,1,2:T(8,128)}), f32[70,8,128]{0,1,2:T(8,128)S(1)}, u32[]{:S(2)}, u32[]{:S(2)}) async-start(f32[70,8,128]{0,1,2:T(8,128)} %copy.55), calls=%async_computation | async-start | bytes 1048576 | tf_op jit(solution)/shard_map/all_to_all | solution.py:192
  29.6 0.7 copy-start.6
  44.8 16.3 %copy-start.2 = (f32[70,70]{1,0:T(8,128)}, f32[70,70]{1,0:T(8,128)S(1)}, u32[]{:S(2)}) copy-start(f32[70,70]{1,0:T(8,128)S(1)} %fusion.72) | copy-start | bytes 58804
  44.8 16.2 %copy-start.5 = (f32[70,8,128]{2,1,0:T(8,128)S(1)}, f32[70,8,128]{2,1,0:T(8,128)}, u32[]{:S(2)}) copy-start(f32[70,8,128]{2,1,0:T(8,128)} %param.10) | copy-start | bytes 860164
  62.0 15.8 %collective-permute-start.2 = (f32[70,8,1]{2,1,0:T(8,128)S(1)}, f32[70,8,1]{2,1,0:T(8,128)S(1)}, u32[]{:S(2)}, u32[]{:S(2)}) collective-permute-start(f32[70,8,1]{2,1,0:T(8,128)S(1)} %get-tuple-element.67), channel_id=1, source_target_pairs={{0,1},{1,2},{2,3},{3,0},{4,5},{5,6},{6,7},{7,4},{8,9},{9,10},{10,1... | collective-permute-start | bytes 6728 | tf_op jit(solution)/shard_map/ppermute | solution.py:25
  70.1 10.9 %collective-permute-start.3 = (f32[70,8,1]{2,1,0:T(8,128)S(1)}, f32[70,8,1]{2,1,0:T(8,128)S(1)}, u32[]{:S(2)}, u32[]{:S(2)}) collective-permute-start(f32[70,8,1]{2,1,0:T(8,128)S(1)} %get-tuple-element.68), channel_id=1, source_target_pairs={{1,0},{2,1},{3,2},{0,3},{5,4},{6,5},{7,6},{4,7},{9,8},{10,9},{11,1... | collective-permute-start | bytes 6728 | tf_op jit(solution)/shard_map/ppermute | solution.py:26
  72.0 9.1 %collective-permute-start = (f32[70,1,128]{2,1,0:T(1,128)S(1)}, f32[70,1,128]{2,1,0:T(1,128)S(1)}, u32[]{:S(2)}, u32[]{:S(2)}) collective-permute-start(f32[70,1,128]{2,1,0:T(1,128)S(1)} %get-tuple-element.65), channel_id=1, source_target_pairs={{4,0},{8,4},{12,8},{16,12},{20,16},{24,20},{28,24},{32,28},{36,32}... | collective-permute-start | bytes 107528 | tf_op jit(solution)/shard_map/ppermute | solution.py:26
  75.6 5.6 collective-permute-start.1
  77.8 3.3 copy-start
  332.2 6.9 %copy-start.1 = (f32[70,8,128]{2,1,0:T(8,128)S(1)}, f32[70,8,128]{2,1,0:T(8,128)}, u32[]{:S(2)}) copy-start(f32[70,8,128]{2,1,0:T(8,128)} %get-tuple-element.56) | copy-start | bytes 860164
  386.8 0.8 copy-start.3
  388.4 16.4 %collective-permute-start.6 = (f32[70,8,1]{2,1,0:T(8,128)S(1)}, f32[70,8,1]{2,1,0:T(8,128)S(1)}, u32[]{:S(2)}, u32[]{:S(2)}) collective-permute-start(f32[70,8,1]{2,1,0:T(8,128)S(1)} %get-tuple-element.61), channel_id=1, source_target_pairs={{0,1},{1,2},{2,3},{3,0},{4,5},{5,6},{6,7},{7,4},{8,9},{9,10},{10,1... | collective-permute-start | bytes 6728 | tf_op jit(solution)/shard_map/ppermute | solution.py:25
  390.3 17.9 %collective-permute-start.7 = (f32[70,8,1]{2,1,0:T(8,128)S(1)}, f32[70,8,1]{2,1,0:T(8,128)S(1)}, u32[]{:S(2)}, u32[]{:S(2)}) collective-permute-start(f32[70,8,1]{2,1,0:T(8,128)S(1)} %get-tuple-element.62), channel_id=1, source_target_pairs={{1,0},{2,1},{3,2},{0,3},{5,4},{6,5},{7,6},{4,7},{9,8},{10,9},{11,1... | collective-permute-start | bytes 6728 | tf_op jit(solution)/shard_map/ppermute | solution.py:26
  395.5 0.7 copy-start.7
  396.4 12.0 %collective-permute-start.4 = (f32[70,1,128]{2,1,0:T(1,128)S(1)}, f32[70,1,128]{2,1,0:T(1,128)S(1)}, u32[]{:S(2)}, u32[]{:S(2)}) collective-permute-start(f32[70,1,128]{2,1,0:T(1,128)S(1)} %get-tuple-element.59), channel_id=1, source_target_pairs={{4,0},{8,4},{12,8},{16,12},{20,16},{24,20},{28,24},{32,28},{36,32}... | collective-permute-start | bytes 107528 | tf_op jit(solution)/shard_map/ppermute | solution.py:26
  401.3 7.1 %collective-permute-start.5 = (f32[70,1,128]{2,1,0:T(1,128)S(1)}, f32[70,1,128]{2,1,0:T(1,128)S(1)}, u32[]{:S(2)}, u32[]{:S(2)}) collective-permute-start(f32[70,1,128]{2,1,0:T(1,128)S(1)} %get-tuple-element.60), channel_id=1, source_target_pairs={{0,4},{4,8},{8,12},{12,16},{16,20},{20,24},{24,28},{28,32},{32,36}... | collective-permute-start | bytes 107528 | tf_op jit(solution)/shard_map/ppermute | solution.py:25
  581.6 39.9 %all-to-all-start.1 = ((f32[64,2,70,8,1]{2,3,1,4,0:T(8,128)}), f32[64,2,70,8,1]{2,3,1,4,0:T(8,128)S(1)}, u32[]{:S(2)}, u32[]{:S(2)}) async-start(f32[64,2,70,8,1]{2,3,1,4,0:T(8,128)} %bitcast.116), calls=%async_computation.1 | async-start | bytes 1048576 | tf_op jit(solution)/shard_map/all_to_all | solution.py:69
where the time goes:
time: 639 us; the launch traced here: 631 us
  blocking collectives  303 us (47%)
  other arithmetic  158 us (25%)
  starting transfers between devices  63 us (10%)
  waiting for transfers between devices  51.3 us (8%)
  local copies, waits for them, and re-layouts  24.5 us (4%)
  between operations  21 us (3%)
  matrix products  10.3 us (2%)
    unnamed x2, blocking collectives  210 us
    psum x10, blocking collectives, over_axes(): value = lax.psum(value, axis)  85.4 us
    another operation x15, other arithmetic, per_device(): jnp.linalg.cholesky(coarse_matrix(mass_all, tile_count, group_count))  81.7 us
    another operation x6, other arithmetic, per_device(): coarse = jax.scipy.linalg.cho_solve((factor, True), sums_all)  40.3 us
    all_to_all x1, waiting for transfers between devices, exchange_in_order(): result = lax.all_to_all(result, axes[k], k, k, tiled=True)  28.8 us
    all_to_all x1, starting transfers between devices, per_device(): lax.all_to_all(column_heating, TILE, split_axis=2, concat_axis=2, tiled=T...  23 us
    all_to_all x1, waiting for transfers between devices, per_device(): lax.all_to_all(column_heating, TILE, split_axis=2, concat_axis=2, tiled=T...  15.9 us
    ppermute x4, starting transfers between devices, padded_2(): lax.ppermute(first, axis, [(b, a) for a, b in up])  15.5 us
  transfers between devices with their start and end apart: 10, of which 4 were waited for; matrix products, arithmetic and copies ran while one was open for 3% of the time, Pallas kernels for 0%

commit v1 on v0

v1 whole, which is shorter than its diff:
```python
import math

import jax
import jax.numpy as jnp
from jax import lax
from jax.experimental import pallas as pl
from jax.experimental.pallas import tpu as pltpu
from jax.sharding import PartitionSpec as P

LV = 70
PX = 8
CY = 128
NG = 4
DIMS = (4, 4, 4, 2)
NT = 128
LP = 80
NCH = LP // 16
UNROLL = 10
NM = 16
GP = 8
F32 = jnp.float32
MESH = pl.DeviceIdType.MESH


def iota(shape, dim):
    return lax.broadcasted_iota(jnp.int32, shape, dim)


def roll(value, shift, axis):
    return pltpu.roll(value, shift, axis)


def blocked(levels, body, init, reverse=False):
    def trip(b, carry):
        for j in range(UNROLL):
            k = b * UNROLL + j
            carry = body(levels - 1 - k if reverse else k, carry)
        return carry

    return lax.fori_loop(0, levels // UNROLL, trip, init)


def total(value):
    return jnp.sum(jnp.sum(value, axis=0, keepdims=True), axis=1, keepdims=True)


def matmul4(left, right):
    out = []
    for j in range(NG):
        term = left[0] * right[j][0:1, :]
        for l in range(1, NG):
            term = term + left[l] * right[j][l : l + 1, :]
        out.append(term)
    return out


def inverse4(columns):
    columns = list(columns)
    row = iota((GP, NT), 0)
    for k in range(NG):
        pivot = 1.0 / columns[k][k : k + 1, :]
        for j in range(NG):
            if j != k:
                scaled = columns[j][k : k + 1, :] * pivot
                columns[j] = jnp.where(row == k, scaled, columns[j] - columns[k] * scaled)
        columns[k] = jnp.where(row == k, pivot, -columns[k] * pivot)
    return columns


def matvec4(columns, vector):
    out = columns[0] * vector[0:1, :]
    for l in range(1, NG):
        out = out + columns[l] * vector[l : l + 1, :]
    return out


def kernel(
    fv,
    sh,
    kel,
    link,
    longwave,
    shortwave,
    out_field,
    out_rad,
    down,
    upw,
    lco,
    cco,
    res,
    smooth0,
    smooth1,
    image,
    hs,
    hr,
    xs,
    xr,
    west_send,
    east_send,
    south_send,
    north_send,
    west_recv,
    east_recv,
    south_recv,
    north_recv,
    zbuf,
    pbuf,
    alpha_co,
    gamma_co,
    last_co,
    line_count,
    row_count,
    a2a_send_sem,
    a2a_recv_sem,
    halo_send_sem,
    halo_recv_sem,
    z_send_sem,
    z_recv_sem,
    p_send_sem,
    p_recv_sem,
):
    ny, nzh, nx, nc = DIMS
    nz = nzh * NG
    np_ = ny * nx * nc
    t = lax.axis_index("tile")
    g = lax.axis_index("grp")
    c = lax.rem(t, nc)
    x = lax.rem(lax.div(t, nc), nx)
    zh = lax.rem(lax.div(t, nc * nx), nzh)
    y = lax.div(t, nc * nx * nzh)
    z = zh * NG + g
    p = (y * nx + x) * nc + c

    def tile_of(y_, zh_, x_, c_):
        return ((y_ * nzh + zh_) * nx + x_) * nc + c_

    def a2a_peer(j):
        dz = lax.rem(j, nzh)
        rest = lax.div(j, nzh)
        dc = lax.rem(rest, nc)
        rest = lax.div(rest, nc)
        dx = lax.rem(rest, nx)
        dy = lax.div(rest, nx)
        return tile_of(
            lax.rem(y + dy, ny), lax.rem(zh + dz, nzh), lax.rem(x + dx, nx), lax.rem(c + dc, nc)
        )

    def z_peer(k):
        z2 = lax.rem(z + k, nz)
        return tile_of(y, lax.div(z2, NG), x, c), lax.rem(z2, NG)

    def p_peer(k):
        p2 = lax.rem(p + k, np_)
        return tile_of(lax.div(p2, nx * nc), zh, lax.rem(lax.div(p2, nc), nx), lax.rem(p2, nc))

    barrier = pltpu.get_barrier_semaphore()

    def greet_tile(j, _):
        pl.semaphore_signal(barrier, inc=1, device_id=(a2a_peer(j), g), device_id_type=MESH)
        return 0

    def greet_grp(j, _):
        dzh = lax.rem(j, nzh)
        dg = lax.div(j, nzh) + 1
        pl.semaphore_signal(
            barrier,
            inc=1,
            device_id=(tile_of(y, lax.rem(zh + dzh, nzh), x, c), lax.rem(g + dg, NG)),
            device_id_type=MESH,
        )
        return 0

    lax.fori_loop(1, NT, greet_tile, 0)
    lax.fori_loop(0, (NG - 1) * nzh, greet_grp, 0)

    def wait_lines(sem):
        pltpu.make_async_copy(line_count, line_count, sem).wait()

    def wait_rows(sem):
        rows = row_count.at[pl.ds(0, nz - 1)]
        pltpu.make_async_copy(rows, rows, sem).wait()

    def a2a_start(src, dst, which):
        def send(j, _):
            peer = a2a_peer(j)
            pltpu.make_async_remote_copy(
                src_ref=src.at[pl.ds(peer, 1), :],
                dst_ref=dst.at[pl.ds(t, 1), :],
                send_sem=a2a_send_sem.at[which],
                recv_sem=a2a_recv_sem.at[which],
                device_id=(peer, g),
                device_id_type=MESH,
            ).start()
            return 0

        lax.fori_loop(1, NT, send, 0)

    def a2a_wait(which):
        wait_lines(a2a_recv_sem.at[which])

    def a2a_drain(which):
        wait_lines(a2a_send_sem.at[which])

    lane = iota((PX, CY), 1)
    row8 = iota((PX, CY), 0)

    def pack_row(values):
        rows = [jnp.sum(v, axis=0, keepdims=True) for v in values]
        rows = rows + [jnp.zeros((1, CY), F32)] * (NM - len(rows))
        sums = jnp.sum(jnp.concatenate(rows, axis=0), axis=1, keepdims=True)
        diag = iota((NM, 128), 0) == iota((NM, 128), 1)
        return jnp.sum(jnp.where(diag, sums, 0.0), axis=0, keepdims=True)

    def gather_start(which, row):
        buf = zbuf.at[which]
        buf[pl.ds(z, 1), :] = row

        def send(k, _):
            pltpu.make_async_remote_copy(
                src_ref=buf.at[pl.ds(z, 1), :],
                dst_ref=buf.at[pl.ds(z, 1), :],
                send_sem=z_send_sem.at[which],
                recv_sem=z_recv_sem.at[which],
                device_id=z_peer(k),
                device_id_type=MESH,
            ).start()
            return 0

        lax.fori_loop(1, nz, send, 0)

    def gather_middle(which):
        buf = zbuf.at[which]
        wait_rows(z_recv_sem.at[which])
        value = buf[...]
        ln = iota((nz, 128), 1)
        mine = lax.rem(ln, nz) == iota((nz, 128), 0)
        packed = []
        for r in range(NM // 8):
            spread = jnp.take_along_axis(value, lax.rem(r * 8 + lax.div(ln, nz), 128), axis=1)
            packed.append(jnp.sum(jnp.where(mine, spread, 0.0), axis=0, keepdims=True))
        pbuf[which, pl.ds(p, 1)] = jnp.concatenate(packed, axis=0)[None]
        dst = pbuf.at[which]

        def send(k, _):
            pltpu.make_async_remote_copy(
                src_ref=dst.at[pl.ds(p, 1)],
                dst_ref=dst.at[pl.ds(p, 1)],
                send_sem=p_send_sem.at[which],
                recv_sem=p_recv_sem.at[which],
                device_id=(p_peer(k), g),
                device_id_type=MESH,
            ).start()
            return 0

        lax.fori_loop(1, np_, send, 0)

    def gather_end(which, count):
        rows = pbuf.at[which, pl.ds(0, np_ - 1)]
        pltpu.make_async_copy(rows, rows, p_recv_sem.at[which]).wait()
        parts = [pbuf[which, :, r, :] for r in range(NM // 8)]
        parts.append(jnp.zeros((128 - np_ * (NM // 8), 128), F32))
        flat = jnp.concatenate(parts, axis=0).T
        ln = iota((128, 128), 1)
        rw = iota((128, 128), 0)
        t_p = (lax.rem(lax.div(ln, nc * nx * nzh), ny) * nx * nc) + lax.rem(ln, nx * nc)
        t_zh = lax.rem(lax.div(ln, nc * nx), nzh)
        keep = lax.div(lax.rem(rw, nz), NG) == t_zh
        found = []
        for r in range(NM // 8):
            if len(found) >= count:
                break
            got = jnp.take_along_axis(flat, t_p + r * np_, axis=1)
            got = jnp.where(keep, got, 0.0)
            for m in range(8):
                if len(found) >= count:
                    break
                block = got[m * nz : (m + 1) * nz, :NT]
                acc = block[0:NG]
                for b in range(1, nzh):
                    acc = acc + block[b * NG : (b + 1) * NG]
                found.append(jnp.concatenate([acc, jnp.zeros((GP - NG, NT), F32)], axis=0))
        return found

    def gather_drain(which):
        wait_rows(z_send_sem.at[which])
        rows = pbuf.at[which, pl.ds(0, np_ - 1)]
        pltpu.make_async_copy(rows, rows, p_send_sem.at[which]).wait()

    zeros = jnp.zeros((PX, CY), F32)
    latitude = ((g * CY + t).astype(F32) + 0.5) / float(CY * NG) - 0.5
    mu10 = 10.0 * jnp.cos(jnp.full((PX, CY), latitude * (math.pi / 2) - 0.4, F32))

    def emission(k):
        square = kel[k] * kel[k]
        return square * square

    def both_passes(k, carry):
        flux_down, flux_up, sun, acc = carry
        em = emission(k)
        trans = jnp.exp(jnp.full((PX, CY), -longwave[k], F32))
        absorbed = 1.0 - trans
        sun_trans = jnp.exp(jnp.full((PX, CY), -shortwave[k], F32))
        raw = absorbed * (flux_down - 2.0 * em) + mu10 * (sun * (1.0 - sun_trans))
        down[k] = raw
        flux_down = trans * flux_down + absorbed * em
        sun = sun * sun_trans
        k2 = LV - 1 - k
        em2 = emission(k2)
        trans2 = jnp.exp(jnp.full((PX, CY), -longwave[k2], F32))
        absorbed2 = 1.0 - trans2
        raw2 = absorbed2 * flux_up
        upw[k2] = raw2
        flux_up = trans2 * flux_up + absorbed2 * em2
        return flux_down, flux_up, sun, acc + (raw + raw2)

    carry = blocked(LV, both_passes, (zeros, emission(LV - 1), jnp.ones((PX, CY), F32), zeros))
    mean = carry[3] * (1.0 / LV)
    for k in range(LV, LP):
        down[k] = zeros
        upw[k] = zeros
        res[k] = zeros
    for ch in range(NCH):
        lv = slice(ch * 16, (ch + 1) * 16)
        heat = down[lv] + upw[lv] - mean[None]
        hs[:, ch * 128 : (ch + 1) * 128] = heat.reshape(16 * PX, CY).T

    def factor(k, carry):
        link_above, inv_above = carry
        here = jnp.where(k < LV - 1, link[jnp.minimum(k, LV - 2)], 0.0)
        here = jnp.full((PX, CY), here, F32)
        low = link_above * inv_above
        inv = 1.0 / (4.0 + here + link_above - link_above * low)
        lco[k] = low
        cco[k] = inv
        return here, inv

    blocked(LV, factor, (zeros, zeros))
    lco[LV] = zeros

    def shift_sums(k, carry):
        v = sh[k]
        return carry[0] + v, carry[1] + v * v

    sh_sum, sh_sq = blocked(LV, shift_sums, (zeros, zeros))
    edge_w = row8 == 0
    edge_e = row8 == PX - 1
    edge_s = lane == 0
    edge_n = lane == CY - 1

    def edges(v):
        return [jnp.where(m, v, 0.0) for m in (edge_w, edge_e, edge_s, edge_n)]

    shift_row = pack_row([sh_sum, sh_sq] + edges(sh_sum))

    pl.semaphore_wait(barrier, NT - 1 + (NG - 1) * nzh)

    gather_start(0, shift_row)
    a2a_start(hs, hr, 0)
    hr[pl.ds(t, 1), :] = hs[pl.ds(t, 1), :]
    gather_middle(0)

    mass, m_ss, m_sw, m_se, m_sso, m_sn = gather_end(0, 6)
    grow = iota((GP, NT), 0)
    gcol = iota((GP, NT), 1)
    live_s = ((grow > 0) & (grow < NG)).astype(F32)
    live_n = (grow < NG - 1).astype(F32)
    diagonal = mass + 2.0 * LV * CY + LV * PX * (live_s + live_n)
    couple = float(LV * CY)
    b_co = []
    a_co = []
    for j in range(NG):
        entry = jnp.where(grow == j, diagonal, 0.0)
        near = (grow == j - 1) | (grow == j + 1)
        entry = jnp.where(near & (grow < NG), -float(LV * PX), entry)
        b_co.append(entry)
        a_co.append(jnp.where(grow == j, -couple, 0.0))

    def reduce_step(step, carry):
        hop, a_, b_, c_ = carry
        back = NT - hop
        binv = inverse4(b_)
        alpha = matmul4(a_, [roll(v, hop, 1) for v in binv])
        gamma = matmul4(c_, [roll(v, back, 1) for v in binv])
        alpha = [-v for v in alpha]
        gamma = [-v for v in gamma]
        a_m = [roll(v, hop, 1) for v in a_]
        c_m = [roll(v, hop, 1) for v in c_]
        a_p = [roll(v, back, 1) for v in a_]
        c_p = [roll(v, back, 1) for v in c_]
        ac = matmul4(alpha, c_m)
        ga = matmul4(gamma, a_p)
        b_ = [b_[j] + ac[j] + ga[j] for j in range(NG)]
        a_ = matmul4(alpha, a_m)
        c_ = matmul4(gamma, c_p)
        for j in range(NG):
            alpha_co[step, j] = alpha[j]
            gamma_co[step, j] = gamma[j]
        return hop * 2, tuple(a_), tuple(b_), tuple(c_)

    steps = int(math.log2(NT))
    _, a_f, b_f, c_f = lax.fori_loop(
        0, steps, reduce_step, (jnp.int32(1), tuple(a_co), tuple(b_co), tuple(a_co))
    )
    last = inverse4([a_f[j] + b_f[j] + c_f[j] for j in range(NG)])
    for j in range(NG):
        last_co[j] = last[j]

    def coarse_solve(rhs):
        for step in range(steps):
            hop = 1 << step
            low = roll(rhs, hop, 1)
            high = roll(rhs, NT - hop, 1)
            rhs = (
                rhs
                + matvec4([alpha_co[step, j] for j in range(NG)], low)
                + matvec4([gamma_co[step, j] for j in range(NG)], high)
            )
        return matvec4([last_co[j] for j in range(NG)], rhs)

    def differences(e):
        return (
            e - roll(e, 1, 1),
            e - roll(e, NT - 1, 1),
            live_s * (e - roll(e, 1, 0)),
            live_n * (e - roll(e, GP - 1, 0)),
        )

    mine = (grow == g) & (gcol == t)

    def own(v):
        return total(jnp.where(mine, v, 0.0))

    def rim_of(w):
        west, east, south, north = (own(v) for v in w)
        return (
            jnp.where(edge_w, west, 0.0)
            + jnp.where(edge_e, east, 0.0)
            + jnp.where(edge_s, south, 0.0)
            + jnp.where(edge_n, north, 0.0)
        )

    long_rim = float(LV * CY)
    short_rim = float(LV * PX)
    corner = float(LV)
    m_shift = (m_sw, m_se, m_sso, m_sn)

    def own_square(e, w):
        cross = (w[0] + w[1]) * (w[2] + w[3])
        value = e * e * m_ss + long_rim * (w[0] * w[0] + w[1] * w[1])
        value = value + short_rim * (w[2] * w[2] + w[3] * w[3]) + 2.0 * corner * cross
        for i in range(4):
            value = value + 2.0 * e * w[i] * m_shift[i]
        return value

    def against(e, w, with_shift, with_edges):
        value = e * with_shift
        for i in range(4):
            value = value + w[i] * with_edges[i]
        return value

    def column_solve(source, dst):
        def forward(k, above):
            value = source(k) + lco[k] * above
            dst[k] = value
            return value

        blocked(LV, forward, zeros)

        def backward(k, carry):
            below, to_south, to_north = carry
            value = cco[k] * dst[k] + lco[k + 1] * below
            dst[k] = value
            to_south = jnp.where(lane == k, roll(value, k, 1), to_south)
            to_north = jnp.where(lane == k, roll(value, lax.rem(k + 1, CY), 1), to_north)
            return value, to_south, to_north

        return blocked(LV, backward, (zeros, zeros, zeros), reverse=True)

    def halo_copies(n):
        left = (lax.rem(t + NT - 1, NT), g)
        right = (lax.rem(t + 1, NT), g)
        below = (t, lax.rem(g + NG - 1, NG))
        above = (t, lax.rem(g + 1, NG))
        table = (
            (west_send, east_recv, left),
            (east_send, west_recv, right),
            (south_send, north_recv, below),
            (north_send, south_recv, above),
        )
        return [
            pltpu.make_async_remote_copy(
                src_ref=src.at[n],
                dst_ref=dst.at[n],
                send_sem=halo_send_sem.at[n, i],
                recv_sem=halo_recv_sem.at[n, i],
                device_id=device,
                device_id_type=MESH,
            )
            for i, (src, dst, device) in enumerate(table)
        ]

    inner_s = edge_s & (g > 0)
    outer_s = edge_s & (g == 0)
    inner_n = edge_n & (g < NG - 1)
    outer_n = edge_n & (g == NG - 1)

    def halo_start(n, field, rims):
        west_send[n] = field[0:LV, 0, :]
        east_send[n] = field[0:LV, PX - 1, :]
        south_send[n] = rims[1]
        north_send[n] = rims[2]
        copies = halo_copies(n)
        for copy in copies:
            copy.start()
        return copies

    def image_level(n, field, k, south_in, north_in):
        v = field[k]
        west = jnp.where(edge_w, west_recv[n, pl.ds(k, 1), :], roll(v, 1, 0))
        east = jnp.where(edge_e, east_recv[n, pl.ds(k, 1), :], roll(v, PX - 1, 0))
        south = jnp.where(inner_s, roll(south_in, lax.rem(CY - k, CY), 1), roll(v, 1, 1))
        south = jnp.where(outer_s, v, south)
        north = jnp.where(inner_n, roll(north_in, CY - 1 - k, 1), roll(v, CY - 1, 1))
        north = jnp.where(outer_n, v, north)
        return res[k] - ((west + east) + (south + north)) + sh[k] * v

    a2a_wait(0)
    for ch in range(NCH):
        top = min(LV, (ch + 1) * 16)
        block = hr[:, ch * 128 : (ch + 1) * 128].T.reshape(16, PX, CY)
        res[ch * 16 : top] = fv[ch * 16 : top] + block[: top - ch * 16]

    rims = column_solve(lambda k: res[k], smooth0)
    halos = halo_start(0, smooth0, rims)
    for copy in halos:
        copy.wait_recv()
    south_in = south_recv[0]
    north_in = north_recv[0]

    def moments0(k, carry):
        r_sum, q_sum, rq, rs, qq, qs = carry
        q = image_level(0, smooth0, k, south_in, north_in)
        image[k] = q
        r = res[k]
        s = sh[k]
        return r_sum + r, q_sum + q, rq + r * q, rs + r * s, qq + q * q, qs + q * s

    r_sum, q_sum, rq, rs, qq, qs = blocked(LV, moments0, (zeros,) * 6)
    gather_start(1, pack_row([r_sum - q_sum, rq, rs, qq, qs] + edges(r_sum) + edges(q_sum)))
    gather_middle(1)
    got = gather_end(1, 13)
    e0 = coarse_solve(got[0])
    w0 = differences(e0)
    m_rq, m_rs, m_qq, m_qs = got[1:5]
    m_re = got[5:9]
    m_qe = got[9:13]
    projection = total(m_rq + against(e0, w0, m_rs, m_re))
    norm0 = total(m_qq + 2.0 * against(e0, w0, m_qs, m_qe) + own_square(e0, w0))
    step0 = projection / norm0
    left_over = projection - step0 * norm0
    i_s = m_qs + against(e0, w0, m_ss, m_shift)
    i_e = (
        m_qe[0] + e0 * m_sw + long_rim * w0[0] + corner * (w0[2] + w0[3]),
        m_qe[1] + e0 * m_se + long_rim * w0[1] + corner * (w0[2] + w0[3]),
        m_qe[2] + e0 * m_sso + short_rim * w0[2] + corner * (w0[0] + w0[1]),
        m_qe[3] + e0 * m_sn + short_rim * w0[3] + corner * (w0[0] + w0[1]),
    )
    e0_own = own(e0)
    rim0 = rim_of(w0)

    def next_residual(k):
        q = image[k] + sh[k] * e0_own + rim0
        image[k] = q
        r = res[k] - step0 * q
        res[k] = r
        return r

    rims = column_solve(next_residual, smooth1)
    halos1 = halo_start(1, smooth1, rims)
    for copy in halos1:
        copy.wait_recv()
    south_in1 = south_recv[1]
    north_in1 = north_recv[1]

    def moments1(k, carry):
        r_sum, q_sum, rq, rs, qq, qs, iq = carry
        q = image_level(1, smooth1, k, south_in1, north_in1)
        r = res[k]
        s = sh[k]
        return (
            r_sum + r,
            q_sum + q,
            rq + r * q,
            rs + r * s,
            qq + q * q,
            qs + q * s,
            iq + image[k] * q,
        )

    r_sum, q_sum, rq, rs, qq, qs, iq = blocked(LV, moments1, (zeros,) * 7)
    gather_start(2, pack_row([r_sum - q_sum, rq, rs, qq, qs] + edges(r_sum) + edges(q_sum) + [iq]))
    gather_middle(2)
    got = gather_end(2, 14)
    e1 = coarse_solve(got[0])
    w1 = differences(e1)
    m_rq, m_rs, m_qq, m_qs = got[1:5]
    m_re = got[5:9]
    m_qe = got[9:13]
    crossing = total(got[13] + against(e1, w1, i_s, i_e))
    projection1 = total(m_rq + against(e1, w1, m_rs, m_re))
    square1 = total(m_qq + 2.0 * against(e1, w1, m_qs, m_qe) + own_square(e1, w1))
    weight = crossing / norm0
    norm1 = square1 - weight * crossing
    step1 = (projection1 - weight * left_over) / norm1
    scale0 = step0 - step1 * weight
    constant = scale0 * e0_own + step1 * own(e1)

    def finish(k, _):
        out_field[k] = scale0 * smooth0[k] + step1 * smooth1[k] + constant
        return 0

    blocked(LV, finish, 0)
    for ch in range(NCH):
        top = min(LV, (ch + 1) * 16)
        block = out_field[ch * 16 : top]
        if top < (ch + 1) * 16:
            block = jnp.concatenate([block, jnp.zeros(((ch + 1) * 16 - top, PX, CY), F32)], axis=0)
        xs[:, ch * 128 : (ch + 1) * 128] = block.reshape(16 * PX, CY).T
    a2a_start(xs, xr, 1)
    xr[pl.ds(t, 1), :] = xs[pl.ds(t, 1), :]
    a2a_wait(1)
    for ch in range(NCH):
        top = min(LV, (ch + 1) * 16)
        block = xr[:, ch * 128 : (ch + 1) * 128].T.reshape(16, PX, CY)
        out_rad[ch * 16 : top] = block[: top - ch * 16]

    a2a_drain(0)
    a2a_drain(1)
    for copy in halos + halos1:
        copy.wait_send()
    for which in range(3):
        gather_drain(which)


def per_device(fv, sh, link, kel, longwave, shortwave):
    vmem = pl.BlockSpec(memory_space=pltpu.VMEM)
    smem = pl.BlockSpec(memory_space=pltpu.SMEM)
    field = jax.ShapeDtypeStruct((LV, PX, CY), F32)
    np_ = DIMS[0] * DIMS[2] * DIMS[3]
    steps = int(math.log2(NT))
    padded = pltpu.VMEM((LP, PX, CY), F32)
    lines = pltpu.VMEM((NT, LP * PX), F32)
    rims = pltpu.VMEM((2, LV, CY), F32)
    corners = pltpu.VMEM((2, PX, CY), F32)
    dma = pltpu.SemaphoreType.DMA
    return pl.pallas_call(
        kernel,
        out_shape=(field, field),
        in_specs=[vmem, vmem, vmem, smem, smem, smem],
        out_specs=(vmem, vmem),
        scratch_shapes=[padded] * 8
        + [lines] * 4
        + [rims, rims, corners, corners, rims, rims, corners, corners]
        + [
            pltpu.VMEM((3, DIMS[1] * NG, 128), F32),
            pltpu.VMEM((3, np_, NM // 8, 128), F32),
            pltpu.VMEM((steps, NG, GP, NT), F32),
            pltpu.VMEM((steps, NG, GP, NT), F32),
            pltpu.VMEM((NG, GP, NT), F32),
            pltpu.VMEM((NT - 1, 1, LP * PX), F32),
            pltpu.VMEM((DIMS[1] * NG, 1, 128), F32),
            dma((2,)),
            dma((2,)),
            dma((2, 4)),
            dma((2, 4)),
            dma((3,)),
            dma((3,)),
            dma((3,)),
            dma((3,)),
        ],
        compiler_params=pltpu.CompilerParams(
            collective_id=0, has_side_effects=True, vmem_limit_bytes=32 << 20
        ),
        name="step",
    )(fv, sh, kel, link, longwave, shortwave)


def solution(mesh):
    spread = P(None, "tile", "grp")
    columns = P(None, None, ("tile", "grp"))
    return jax.shard_map(
        per_device,
        mesh=mesh,
        in_specs=(spread, spread, P(), columns, P(), P()),
        out_specs=(spread, columns),
        check_vma=False,
    )
```

time: 639 us -> 114 us (0.18); the launches traced: 631 us -> 113 us
  blocking collectives: 303 us -> 0 us
  other arithmetic: 158 us -> 0 us
  Pallas kernels: 0 us -> 106 us
  starting transfers between devices: 63 us -> 0 us
  waiting for transfers between devices: 51.3 us -> 0 us
  between operations: 21 us -> 0.65 us
  local copies, waits for them, and re-layouts: 24.5 us -> 6.26 us
  matrix products: 10.3 us -> 0 us
    unnamed x2 -> x0, blocking collectives: 210 us -> none
    another operation x30 -> x0, other arithmetic: 139 us -> none  [the longest x15 81.7 us: per_device(): jnp.linalg.cholesky(coarse_matrix(mass_all, tile_count, group_count))]
    pallas_call x0 -> x1, Pallas kernels: none -> 106 us  [per_device(): pl.pallas_call(kernel, out_shape=(field, field), in_specs=[vmem, vmem, vm...]
    psum x10 -> x0, blocking collectives: 85.4 us -> none  [over_axes(): value = lax.psum(value, axis)]
    all_to_all x2 -> x0, waiting for transfers between devices: 44.7 us -> none  [the longest x1 28.8 us: exchange_in_order(): result = lax.all_to_all(result, axes[k], k, k, tiled=True)]
    all_to_all x2 -> x0, starting transfers between devices: 32 us -> none  [the longest x1 23 us: per_device(): lax.all_to_all(column_heating, TILE, split_axis=2, concat_axis=2, tiled=T...]
    ppermute x8 -> x0, starting transfers between devices: 31 us -> none  [the longest x4 15.5 us: padded_2(): lax.ppermute(first, axis, [(b, a) for a, b in up])]
    another operation x19 -> x0, local copies, waits for them, and re-layouts: 12.3 us -> none  [the longest x13 10.6 us: per_device(): coarse = jax.scipy.linalg.cho_solve((factor, True), sums_all)]
  transfers between devices with their start and end apart: 10 -> 0, of which waited for: 4 -> 0; matrix products, arithmetic and copies ran while one was open for 3% -> 0% of each run, Pallas kernels for 0% -> 0%
where the time goes in v1:
time: 114 us; the launch traced here: 113 us
  Pallas kernels  106 us (93%)
  local copies, waits for them, and re-layouts  6.26 us (5%)
    pallas_call x1, Pallas kernels, per_device(): pl.pallas_call(kernel, out_shape=(field, field), in_specs=[vmem, vmem, vm...  106 us
    unnamed x14, local copies, waits for them, and re-layouts  6.26 us

profile of v1, /device:TPU:1, one launch (start us, length us, event | category | flops | bytes accessed | tf_op | source)
XLA Modules:
  0.0 113.2 jit_solution(3821907491346875350)
XLA Ops:
  0.6 0.0 copy-start
  0.6 0.9 copy-done
  1.6 0.0 copy-start.1
  1.6 1.0 copy-done.1
  2.5 0.0 copy-start.2
  2.6 1.0 copy-done.2
  3.5 0.0 copy-start.3
  3.5 0.7 copy-done.3
  4.2 0.0 copy-start.4
  4.2 0.7 copy-done.4
  4.8 0.0 copy-start.5
  4.8 0.7 copy-done.5
  5.5 106.3 %step.1 = (f32[70,8,128]{2,1,0:T(8,128)S(1)}, f32[70,8,128]{2,1,0:T(8,128)S(1)}) custom-call(f32[70,8,128]{2,1,0:T(8,128)S(1)} %copy-done, f32[70,8,128]{2,1,0:T(8,128)S(1)} %copy-done.1, f32[70,8,128]{2,1,0:T(8,128)S(1)} %copy-done.2, f32[69]{0:T(128)S(1)} %copy-done.3, f32[70]{0:T(128)S(1)} %copy-done.4, f32[70]{0:T(128)S(1)} %copy-done.5), custom_call_target="tpu_custom_call" | custom-call | tf_op jit(solution)/shard_map/step/pallas_call | solution.py:656
  111.8 0.7 copy.10
  112.5 0.7 copy.11
Async XLA Ops:
  0.6 1.0 copy-start
  1.6 1.0 copy-start.1
  2.5 1.0 copy-start.2
  3.5 0.7 copy-start.3
  4.2 0.7 copy-start.4
  4.8 0.7 copy-start.5

commit v2 on v1

--- a/solution.py
+++ b/solution.py
@@ -75,14 +75,20 @@
 
 
 def kernel(
+    fv_hbm,
+    sh_hbm,
+    kel_hbm,
+    link_hbm,
+    longwave_hbm,
+    shortwave_hbm,
+    out_field,
+    out_rad,
     fv,
     sh,
     kel,
     link,
     longwave,
     shortwave,
-    out_field,
-    out_rad,
     down,
     upw,
     lco,
@@ -91,8 +97,12 @@
     smooth0,
     smooth1,
     image,
+    shift_solve,
+    image_solve,
     hs,
     hr,
+    fs,
+    fr,
     xs,
     xr,
     west_send,
@@ -110,6 +120,9 @@
     last_co,
     line_count,
     row_count,
+    ghost_west,
+    ghost_east,
+    in_sem,
     a2a_send_sem,
     a2a_recv_sem,
     halo_send_sem,
@@ -134,44 +147,65 @@
     def tile_of(y_, zh_, x_, c_):
         return ((y_ * nzh + zh_) * nx + x_) * nc + c_
 
-    def a2a_peer(j):
-        dz = lax.rem(j, nzh)
-        rest = lax.div(j, nzh)
-        dc = lax.rem(rest, nc)
-        rest = lax.div(rest, nc)
-        dx = lax.rem(rest, nx)
-        dy = lax.div(rest, nx)
-        return tile_of(
-            lax.rem(y + dy, ny), lax.rem(zh + dz, nzh), lax.rem(x + dx, nx), lax.rem(c + dc, nc)
-        )
-
-    def z_peer(k):
-        z2 = lax.rem(z + k, nz)
-        return tile_of(y, lax.div(z2, NG), x, c), lax.rem(z2, NG)
-
-    def p_peer(k):
-        p2 = lax.rem(p + k, np_)
-        return tile_of(lax.div(p2, nx * nc), zh, lax.rem(lax.div(p2, nc), nx), lax.rem(p2, nc))
+    z_part = [lax.rem(zh + dz, nzh) * (nx * nc) for dz in range(nzh)]
+    z_order = sorted(range(nzh), key=lambda dz: -min(dz, nzh - dz))
+
+    def plane_base(r):
+        dc = lax.rem(r, nc)
+        dx = lax.rem(lax.div(r, nc), nx)
+        dy = lax.div(r, nc * nx)
+        low = lax.rem(x + dx, nx) * nc + lax.rem(c + dc, nc)
+        return lax.rem(y + dy, ny) * (nzh * nx * nc) + low
+
+    def each_tile(low, high, act):
+        if low == 0:
+            base = plane_base(0)
+            for dz in z_order[:-1]:
+                act(base + z_part[dz])
+
+        def some(r, _):
+            base = plane_base(r)
+            for dz in z_order:
+                act(base + z_part[dz])
+            return 0
+
+        lax.fori_loop(max(low, 1), high, some, 0)
+
+    plane_here = plane_base(0)
+
+    def each_z(first, act):
+        if first == 0:
+            for dz in z_order[:-1]:
+                act(plane_here + z_part[dz], g)
+
+        def some(dg, _):
+            g2 = lax.rem(g + dg, NG)
+            for dz in z_order:
+                act(plane_here + z_part[dz], g2)
+            return 0
+
+        lax.fori_loop(1, NG, some, 0)
 
     barrier = pltpu.get_barrier_semaphore()
 
-    def greet_tile(j, _):
-        pl.semaphore_signal(barrier, inc=1, device_id=(a2a_peer(j), g), device_id_type=MESH)
-        return 0
-
-    def greet_grp(j, _):
-        dzh = lax.rem(j, nzh)
-        dg = lax.div(j, nzh) + 1
-        pl.semaphore_signal(
-            barrier,
-            inc=1,
-            device_id=(tile_of(y, lax.rem(zh + dzh, nzh), x, c), lax.rem(g + dg, NG)),
-            device_id_type=MESH,
-        )
-        return 0
-
-    lax.fori_loop(1, NT, greet_tile, 0)
-    lax.fori_loop(0, (NG - 1) * nzh, greet_grp, 0)
+    def greet(tile, grp):
+        pl.semaphore_signal(barrier, inc=1, device_id=(tile, grp), device_id_type=MESH)
+
+    each_z(1, greet)
+    each_tile(0, np_, lambda tile: greet(tile, g))
+    pairs = (
+        (kel_hbm, kel),
+        (longwave_hbm, longwave),
+        (shortwave_hbm, shortwave),
+        (link_hbm, link),
+        (sh_hbm, sh),
+        (fv_hbm, fv.at[pl.ds(0, LV)]),
+    )
+    loads = [pltpu.make_async_copy(src, dst, in_sem.at[i]) for i, (src, dst) in enumerate(pairs)]
+    for load in loads:
+        load.start()
+    for load in loads:
+        load.wait()
 
     def wait_lines(sem):
         pltpu.make_async_copy(line_count, line_count, sem).wait()
@@ -180,9 +214,8 @@
         rows = row_count.at[pl.ds(0, nz - 1)]
         pltpu.make_async_copy(rows, rows, sem).wait()
 
-    def a2a_start(src, dst, which):
-        def send(j, _):
-            peer = a2a_peer(j)
+    def a2a_start(src, dst, which, low, high):
+        def send(peer):
             pltpu.make_async_remote_copy(
                 src_ref=src.at[pl.ds(peer, 1), :],
                 dst_ref=dst.at[pl.ds(t, 1), :],
@@ -191,9 +224,8 @@
                 device_id=(peer, g),
                 device_id_type=MESH,
             ).start()
-            return 0
-
-        lax.fori_loop(1, NT, send, 0)
+
+        each_tile(low, high, send)
 
     def a2a_wait(which):
         wait_lines(a2a_recv_sem.at[which])
@@ -215,18 +247,17 @@
         buf = zbuf.at[which]
         buf[pl.ds(z, 1), :] = row
 
-        def send(k, _):
+        def send(tile, grp):
             pltpu.make_async_remote_copy(
                 src_ref=buf.at[pl.ds(z, 1), :],
                 dst_ref=buf.at[pl.ds(z, 1), :],
                 send_sem=z_send_sem.at[which],
                 recv_sem=z_recv_sem.at[which],
-                device_id=z_peer(k),
+                device_id=(tile, grp),
                 device_id_type=MESH,
             ).start()
-            return 0
-
-        lax.fori_loop(1, nz, send, 0)
+
+        each_z(0, send)
 
     def gather_middle(which):
         buf = zbuf.at[which]
@@ -241,13 +272,13 @@
         pbuf[which, pl.ds(p, 1)] = jnp.concatenate(packed, axis=0)[None]
         dst = pbuf.at[which]
 
-        def send(k, _):
+        def send(r, _):
             pltpu.make_async_remote_copy(
                 src_ref=dst.at[pl.ds(p, 1)],
                 dst_ref=dst.at[pl.ds(p, 1)],
                 send_sem=p_send_sem.at[which],
                 recv_sem=p_recv_sem.at[which],
-                device_id=(p_peer(k), g),
+                device_id=(plane_base(r) + z_part[0], g),
                 device_id_type=MESH,
             ).start()
             return 0
@@ -316,13 +347,29 @@
     carry = blocked(LV, both_passes, (zeros, emission(LV - 1), jnp.ones((PX, CY), F32), zeros))
     mean = carry[3] * (1.0 / LV)
     for k in range(LV, LP):
+        fv[k] = zeros
+        smooth1[k] = zeros
         down[k] = zeros
         upw[k] = zeros
         res[k] = zeros
     for ch in range(NCH):
         lv = slice(ch * 16, (ch + 1) * 16)
         heat = down[lv] + upw[lv] - mean[None]
+        down[lv] = heat
         hs[:, ch * 128 : (ch + 1) * 128] = heat.reshape(16 * PX, CY).T
+
+    def lines_of(field, dst):
+        for ch in range(NCH):
+            dst[:, ch * 128 : (ch + 1) * 128] = (
+                field[ch * 16 : (ch + 1) * 16].reshape(16 * PX, CY).T
+            )
+
+    def columns_of(src, ch):
+        top = min(LV, (ch + 1) * 16)
+        block = src[:, ch * 128 : (ch + 1) * 128].T.reshape(16, PX, CY)
+        return slice(ch * 16, top), block[: top - ch * 16]
+
+    lines_of(fv, fs)
 
     def factor(k, carry):
         link_above, inv_above = carry
@@ -351,112 +398,6 @@
         return [jnp.where(m, v, 0.0) for m in (edge_w, edge_e, edge_s, edge_n)]
 
     shift_row = pack_row([sh_sum, sh_sq] + edges(sh_sum))
-
-    pl.semaphore_wait(barrier, NT - 1 + (NG - 1) * nzh)
-
-    gather_start(0, shift_row)
-    a2a_start(hs, hr, 0)
-    hr[pl.ds(t, 1), :] = hs[pl.ds(t, 1), :]
-    gather_middle(0)
-
-    mass, m_ss, m_sw, m_se, m_sso, m_sn = gather_end(0, 6)
-    grow = iota((GP, NT), 0)
-    gcol = iota((GP, NT), 1)
-    live_s = ((grow > 0) & (grow < NG)).astype(F32)
-    live_n = (grow < NG - 1).astype(F32)
-    diagonal = mass + 2.0 * LV * CY + LV * PX * (live_s + live_n)
-    couple = float(LV * CY)
-    b_co = []
-    a_co = []
-    for j in range(NG):
-        entry = jnp.where(grow == j, diagonal, 0.0)
-        near = (grow == j - 1) | (grow == j + 1)
-        entry = jnp.where(near & (grow < NG), -float(LV * PX), entry)
-        b_co.append(entry)
-        a_co.append(jnp.where(grow == j, -couple, 0.0))
-
-    def reduce_step(step, carry):
-        hop, a_, b_, c_ = carry
-        back = NT - hop
-        binv = inverse4(b_)
-        alpha = matmul4(a_, [roll(v, hop, 1) for v in binv])
-        gamma = matmul4(c_, [roll(v, back, 1) for v in binv])
-        alpha = [-v for v in alpha]
-        gamma = [-v for v in gamma]
-        a_m = [roll(v, hop, 1) for v in a_]
-        c_m = [roll(v, hop, 1) for v in c_]
-        a_p = [roll(v, back, 1) for v in a_]
-        c_p = [roll(v, back, 1) for v in c_]
-        ac = matmul4(alpha, c_m)
-        ga = matmul4(gamma, a_p)
-        b_ = [b_[j] + ac[j] + ga[j] for j in range(NG)]
-        a_ = matmul4(alpha, a_m)
-        c_ = matmul4(gamma, c_p)
-        for j in range(NG):
-            alpha_co[step, j] = alpha[j]
-            gamma_co[step, j] = gamma[j]
-        return hop * 2, tuple(a_), tuple(b_), tuple(c_)
-
-    steps = int(math.log2(NT))
-    _, a_f, b_f, c_f = lax.fori_loop(
-        0, steps, reduce_step, (jnp.int32(1), tuple(a_co), tuple(b_co), tuple(a_co))
-    )
-    last = inverse4([a_f[j] + b_f[j] + c_f[j] for j in range(NG)])
-    for j in range(NG):
-        last_co[j] = last[j]
-
-    def coarse_solve(rhs):
-        for step in range(steps):
-            hop = 1 << step
-            low = roll(rhs, hop, 1)
-            high = roll(rhs, NT - hop, 1)
-            rhs = (
-                rhs
-                + matvec4([alpha_co[step, j] for j in range(NG)], low)
-                + matvec4([gamma_co[step, j] for j in range(NG)], high)
-            )
-        return matvec4([last_co[j] for j in range(NG)], rhs)
-
-    def differences(e):
-        return (
-            e - roll(e, 1, 1),
-            e - roll(e, NT - 1, 1),
-            live_s * (e - roll(e, 1, 0)),
-            live_n * (e - roll(e, GP - 1, 0)),
-        )
-
-    mine = (grow == g) & (gcol == t)
-
-    def own(v):
-        return total(jnp.where(mine, v, 0.0))
-
-    def rim_of(w):
-        west, east, south, north = (own(v) for v in w)
-        return (
-            jnp.where(edge_w, west, 0.0)
-            + jnp.where(edge_e, east, 0.0)
-            + jnp.where(edge_s, south, 0.0)
-            + jnp.where(edge_n, north, 0.0)
-        )
-
-    long_rim = float(LV * CY)
-    short_rim = float(LV * PX)
-    corner = float(LV)
-    m_shift = (m_sw, m_se, m_sso, m_sn)
-
-    def own_square(e, w):
-        cross = (w[0] + w[1]) * (w[2] + w[3])
-        value = e * e * m_ss + long_rim * (w[0] * w[0] + w[1] * w[1])
-        value = value + short_rim * (w[2] * w[2] + w[3] * w[3]) + 2.0 * corner * cross
-        for i in range(4):
-            value = value + 2.0 * e * w[i] * m_shift[i]
-        return value
-
-    def against(e, w, with_shift, with_edges):
-        value = e * with_shift
-        for i in range(4):
-            value = value + w[i] * with_edges[i]
-        return value
 
     def column_solve(source, dst):
         def forward(k, above):
@@ -499,54 +440,188 @@
             for i, (src, dst, device) in enumerate(table)
         ]
 
+    def halo_fill(n, field, rims):
+        west_send[n] = field[0:LV, 0, :]
+        east_send[n] = field[0:LV, PX - 1, :]
+        south_send[n] = rims[1]
+        north_send[n] = rims[2]
+
+    def halo_start(n):
+        copies = halo_copies(n)
+        for copy in copies:
+            copy.start()
+        return copies
+
+    def plain_solve(field, dst):
+        def forward(k, above):
+            value = field[k] + lco[k] * above
+            dst[k] = value
+            return value
+
+        blocked(LV, forward, zeros)
+
+        def backward(k, below):
+            value = cco[k] * dst[k] + lco[k + 1] * below
+            dst[k] = value
+            return value
+
+        blocked(LV, backward, zeros, reverse=True)
+
+    shift_rims = column_solve(lambda k: sh[k], shift_solve)
+    halo_fill(2, shift_solve, shift_rims)
+
+    pl.semaphore_wait(barrier, NT - 1 + (NG - 1) * nzh)
+
+    gather_start(0, shift_row)
+    a2a_start(hs, hr, 0, 0, np_)
+    hr[pl.ds(t, 1), :] = hs[pl.ds(t, 1), :]
+    fr[pl.ds(t, 1), :] = fs[pl.ds(t, 1), :]
+    halos2 = halo_start(2)
+    gather_middle(0)
+
+    mass, m_ss, m_sw, m_se, m_sso, m_sn = gather_end(0, 6)
+    grow = iota((GP, NT), 0)
+    gcol = iota((GP, NT), 1)
+    live_s = ((grow > 0) & (grow < NG)).astype(F32)
+    live_n = (grow < NG - 1).astype(F32)
+    diagonal = mass + 2.0 * LV * CY + LV * PX * (live_s + live_n)
+    couple = float(LV * CY)
+    b_co = []
+    a_co = []
+    for j in range(NG):
+        entry = jnp.where(grow == j, diagonal, 0.0)
+        near = (grow == j - 1) | (grow == j + 1)
+        entry = jnp.where(near & (grow < NG), -float(LV * PX), entry)
+        b_co.append(entry)
+        a_co.append(jnp.where(grow == j, -couple, 0.0))
+
+    def reduce_step(step, carry):
+        hop, a_, b_, c_ = carry
+        back = NT - hop
+        binv = inverse4(b_)
+        alpha = matmul4(a_, [roll(v, hop, 1) for v in binv])
+        gamma = matmul4(c_, [roll(v, back, 1) for v in binv])
+        alpha = [-v for v in alpha]
+        gamma = [-v for v in gamma]
+        a_m = [roll(v, hop, 1) for v in a_]
+        c_m = [roll(v, hop, 1) for v in c_]
+        a_p = [roll(v, back, 1) for v in a_]
+        c_p = [roll(v, back, 1) for v in c_]
+        ac = matmul4(alpha, c_m)
+        ga = matmul4(gamma, a_p)
+        b_ = [b_[j] + ac[j] + ga[j] for j in range(NG)]
+        a_ = matmul4(alpha, a_m)
+        c_ = matmul4(gamma, c_p)
+        for j in range(NG):
+            alpha_co[step, j] = alpha[j]
+            gamma_co[step, j] = gamma[j]
+        return hop * 2, tuple(a_), tuple(b_), tuple(c_)
+
+    steps = int(math.log2(NT))
+    _, a_f, b_f, c_f = lax.fori_loop(
+        0, steps, reduce_step, (jnp.int32(1), tuple(a_co), tuple(b_co), tuple(a_co))
+    )
+    last = inverse4([a_f[j] + b_f[j] + c_f[j] for j in range(NG)])
+    for j in range(NG):
+        last_co[j] = last[j]
+
+    def coarse_solve(rhs):
+        for step in range(steps):
+            hop = 1 << step
+            low = roll(rhs, hop, 1)
+            high = roll(rhs, NT - hop, 1)
+            rhs = (
+                rhs
+                + matvec4([alpha_co[step, j] for j in range(NG)], low)
+                + matvec4([gamma_co[step, j] for j in range(NG)], high)
+            )
+        return matvec4([last_co[j] for j in range(NG)], rhs)
+
+    def differences(e):
+        return (
+            e - roll(e, 1, 1),
+            e - roll(e, NT - 1, 1),
+            live_s * (e - roll(e, 1, 0)),
+            live_n * (e - roll(e, GP - 1, 0)),
+        )
+
+    mine = (grow == g) & (gcol == t)
+
+    def own(v):
+        return total(jnp.where(mine, v, 0.0))
+
+    def rim_of(west, east, south, north):
+        return (
+            jnp.where(edge_w, west, 0.0)
+            + jnp.where(edge_e, east, 0.0)
+            + jnp.where(edge_s, south, 0.0)
+            + jnp.where(edge_n, north, 0.0)
+        )
+
+    long_rim = float(LV * CY)
+    short_rim = float(LV * PX)
+    corner = float(LV)
+    m_shift = (m_sw, m_se, m_sso, m_sn)
+
+    def own_square(e, w):
+        cross = (w[0] + w[1]) * (w[2] + w[3])
+        value = e * e * m_ss + long_rim * (w[0] * w[0] + w[1] * w[1])
+        value = value + short_rim * (w[2] * w[2] + w[3] * w[3]) + 2.0 * corner * cross
+        for i in range(4):
+            value = value + 2.0 * e * w[i] * m_shift[i]
+        return value
+
+    def against(e, w, with_shift, with_edges):
+        value = e * with_shift
+        for i in range(4):
+            value = value + w[i] * with_edges[i]
+        return value
+
     inner_s = edge_s & (g > 0)
     outer_s = edge_s & (g == 0)
     inner_n = edge_n & (g < NG - 1)
     outer_n = edge_n & (g == NG - 1)
 
-    def halo_start(n, field, rims):
-        west_send[n] = field[0:LV, 0, :]
-        east_send[n] = field[0:LV, PX - 1, :]
-        south_send[n] = rims[1]
-        north_send[n] = rims[2]
-        copies = halo_copies(n)
-        for copy in copies:
-            copy.start()
-        return copies
-
-    def image_level(n, field, k, south_in, north_in):
-        v = field[k]
-        west = jnp.where(edge_w, west_recv[n, pl.ds(k, 1), :], roll(v, 1, 0))
-        east = jnp.where(edge_e, east_recv[n, pl.ds(k, 1), :], roll(v, PX - 1, 0))
+    def image_level(v, r, k, west_in, east_in, south_in, north_in):
+        west = jnp.where(edge_w, west_in[pl.ds(k, 1), :], roll(v, 1, 0))
+        east = jnp.where(edge_e, east_in[pl.ds(k, 1), :], roll(v, PX - 1, 0))
         south = jnp.where(inner_s, roll(south_in, lax.rem(CY - k, CY), 1), roll(v, 1, 1))
         south = jnp.where(outer_s, v, south)
         north = jnp.where(inner_n, roll(north_in, CY - 1 - k, 1), roll(v, CY - 1, 1))
         north = jnp.where(outer_n, v, north)
-        return res[k] - ((west + east) + (south + north)) + sh[k] * v
+        return r - ((west + east) + (south + north)) + sh[k] * v
 
     a2a_wait(0)
     for ch in range(NCH):
-        top = min(LV, (ch + 1) * 16)
-        block = hr[:, ch * 128 : (ch + 1) * 128].T.reshape(16, PX, CY)
-        res[ch * 16 : top] = fv[ch * 16 : top] + block[: top - ch * 16]
-
+        lv, block = columns_of(hr, ch)
+        res[lv] = fv[lv] + block
+
+    half = np_ // 2
     rims = column_solve(lambda k: res[k], smooth0)
-    halos = halo_start(0, smooth0, rims)
-    for copy in halos:
+    halo_fill(0, smooth0, rims)
+    halos0 = halo_start(0)
+    a2a_start(fs, fr, 1, 0, half)
+    for copy in halos0:
         copy.wait_recv()
     south_in = south_recv[0]
     north_in = north_recv[0]
 
     def moments0(k, carry):
         r_sum, q_sum, rq, rs, qq, qs = carry
-        q = image_level(0, smooth0, k, south_in, north_in)
+        r = res[k]
+        q = image_level(
+            smooth0[k], r, k, west_recv.at[0], east_recv.at[0], south_in, north_in
+        )
         image[k] = q
-        r = res[k]
         s = sh[k]
         return r_sum + r, q_sum + q, rq + r * q, rs + r * s, qq + q * q, qs + q * s
 
     r_sum, q_sum, rq, rs, qq, qs = blocked(LV, moments0, (zeros,) * 6)
     gather_start(1, pack_row([r_sum - q_sum, rq, rs, qq, qs] + edges(r_sum) + edges(q_sum)))
+    image_rims = column_solve(lambda k: image[k], image_solve)
+    halo_fill(1, image_solve, image_rims)
+    halos1 = halo_start(1)
+    a2a_start(fs, fr, 1, half, np_)
     gather_middle(1)
     got = gather_end(1, 13)
     e0 = coarse_solve(got[0])
@@ -565,28 +640,52 @@
         m_qe[2] + e0 * m_sso + short_rim * w0[2] + corner * (w0[0] + w0[1]),
         m_qe[3] + e0 * m_sn + short_rim * w0[3] + corner * (w0[0] + w0[1]),
     )
-    e0_own = own(e0)
-    rim0 = rim_of(w0)
-
-    def next_residual(k):
-        q = image[k] + sh[k] * e0_own + rim0
-        image[k] = q
-        r = res[k] - step0 * q
-        res[k] = r
-        return r
-
-    rims = column_solve(next_residual, smooth1)
-    halos1 = halo_start(1, smooth1, rims)
-    for copy in halos1:
+    at_west = (grow == g) & (gcol == lax.rem(t + NT - 1, NT))
+    at_east = (grow == g) & (gcol == lax.rem(t + 1, NT))
+    at_south = (grow == g - 1) & (gcol == t)
+    at_north = (grow == g + 1) & (gcol == t)
+    wanted = [(m, e0) for m in (mine, at_west, at_east, at_south, at_north)]
+    wanted = wanted + [(mine, v) for v in w0]
+    wanted = wanted + [(at_west, w0[i]) for i in (1, 2, 3)]
+    wanted = wanted + [(at_east, w0[i]) for i in (0, 2, 3)]
+    wanted = wanted + [(at_south, w0[i]) for i in (3, 0, 1)]
+    wanted = wanted + [(at_north, w0[i]) for i in (2, 0, 1)]
+    found = [jnp.sum(jnp.where(m, v, 0.0), axis=0, keepdims=True) for m, v in wanted]
+    found = found + [jnp.zeros((1, NT), F32)] * (24 - len(found))
+    found = jnp.sum(jnp.concatenate(found, axis=0), axis=1, keepdims=True)
+    found = [found[i : i + 1] for i in range(21)]
+    e0_own, e_west, e_east, e_south, e_north = found[0:5]
+    rim0 = rim_of(*found[5:9])
+    lane1 = iota((1, CY), 1)
+    row1 = iota((PX, 1), 0)
+
+    def rim_row(f):
+        return f[0] + jnp.where(lane1 == 0, f[1], 0.0) + jnp.where(lane1 == CY - 1, f[2], 0.0)
+
+    def rim_col(f):
+        return f[0] + jnp.where(row1 == 0, f[1], 0.0) + jnp.where(row1 == PX - 1, f[2], 0.0)
+
+    for copy in halos2 + halos1:
         copy.wait_recv()
-    south_in1 = south_recv[1]
-    north_in1 = north_recv[1]
+
+    def ghost(recv, e, rim):
+        return recv[0] - step0 * (recv[1] + e * recv[2] + 0.25 * rim)
+
+    ghost_west[...] = ghost(west_recv, e_west, rim_row(found[9:12]))
+    ghost_east[...] = ghost(east_recv, e_east, rim_row(found[12:15]))
+    ghost_south = ghost(south_recv, e_south, rim_col(found[15:18]))
+    ghost_north = ghost(north_recv, e_north, rim_col(found[18:21]))
+
+    quarter_rim = 0.25 * rim0
 
     def moments1(k, carry):
         r_sum, q_sum, rq, rs, qq, qs, iq = carry
-        q = image_level(1, smooth1, k, south_in1, north_in1)
-        r = res[k]
         s = sh[k]
+        q0 = image[k] + s * e0_own + rim0
+        r = res[k] - step0 * q0
+        v = smooth0[k] - step0 * (image_solve[k] + e0_own * shift_solve[k] + quarter_rim)
+        smooth1[k] = v
+        q = image_level(v, r, k, ghost_west, ghost_east, ghost_south, ghost_north)
         return (
             r_sum + r,
             q_sum + q,
@@ -594,12 +693,23 @@
             rs + r * s,
             qq + q * q,
             qs + q * s,
-            iq + image[k] * q,
+            iq + q0 * q,
         )
 
     r_sum, q_sum, rq, rs, qq, qs, iq = blocked(LV, moments1, (zeros,) * 7)
     gather_start(2, pack_row([r_sum - q_sum, rq, rs, qq, qs] + edges(r_sum) + edges(q_sum) + [iq]))
+    lines_of(smooth1, xs)
+    a2a_start(xs, xr, 2, 0, half)
+    xr[pl.ds(t, 1), :] = xs[pl.ds(t, 1), :]
+
+    a2a_wait(1)
+    for ch in range(NCH):
+        lv, block = columns_of(fr, ch)
+        down[lv] = down[lv] + block
+    plain_solve(down, upw)
+
     gather_middle(2)
+    a2a_start(xs, xr, 2, half, np_)
     got = gather_end(2, 14)
     e1 = coarse_solve(got[0])
     w1 = differences(e1)
@@ -613,53 +723,49 @@
     norm1 = square1 - weight * crossing
     step1 = (projection1 - weight * left_over) / norm1
     scale0 = step0 - step1 * weight
-    constant = scale0 * e0_own + step1 * own(e1)
+    block_part = scale0 * e0 + step1 * e1
+    constant = own(block_part)
+    by_tile = jnp.sum(jnp.where(grow == g, block_part, 0.0), axis=0, keepdims=True)
 
     def finish(k, _):
         out_field[k] = scale0 * smooth0[k] + step1 * smooth1[k] + constant
         return 0
 
     blocked(LV, finish, 0)
+
+    a2a_wait(2)
     for ch in range(NCH):
-        top = min(LV, (ch + 1) * 16)
-        block = out_field[ch * 16 : top]
-        if top < (ch + 1) * 16:
-            block = jnp.concatenate([block, jnp.zeros(((ch + 1) * 16 - top, PX, CY), F32)], axis=0)
-        xs[:, ch * 128 : (ch + 1) * 128] = block.reshape(16 * PX, CY).T
-    a2a_start(xs, xr, 1)
-    xr[pl.ds(t, 1), :] = xs[pl.ds(t, 1), :]
-    a2a_wait(1)
-    for ch in range(NCH):
-        top = min(LV, (ch + 1) * 16)
-        block = xr[:, ch * 128 : (ch + 1) * 128].T.reshape(16, PX, CY)
-        out_rad[ch * 16 : top] = block[: top - ch * 16]
-
-    a2a_drain(0)
-    a2a_drain(1)
-    for copy in halos + halos1:
+        lv, block = columns_of(xr, ch)
+        out_rad[lv] = scale0 * upw[lv] + step1 * block + by_tile[None]
+
+    for which in range(3):
+        a2a_drain(which)
+        gather_drain(which)
+    for copy in halos0 + halos1 + halos2:
         copy.wait_send()
-    for which in range(3):
-        gather_drain(which)
 
 
 def per_device(fv, sh, link, kel, longwave, shortwave):
     vmem = pl.BlockSpec(memory_space=pltpu.VMEM)
-    smem = pl.BlockSpec(memory_space=pltpu.SMEM)
+    hbm = pl.BlockSpec(memory_space=pltpu.HBM)
     field = jax.ShapeDtypeStruct((LV, PX, CY), F32)
     np_ = DIMS[0] * DIMS[2] * DIMS[3]
     steps = int(math.log2(NT))
     padded = pltpu.VMEM((LP, PX, CY), F32)
+    whole = pltpu.VMEM((LV, PX, CY), F32)
     lines = pltpu.VMEM((NT, LP * PX), F32)
-    rims = pltpu.VMEM((2, LV, CY), F32)
-    corners = pltpu.VMEM((2, PX, CY), F32)
+    rims = pltpu.VMEM((3, LV, CY), F32)
+    corners = pltpu.VMEM((3, PX, CY), F32)
     dma = pltpu.SemaphoreType.DMA
     return pl.pallas_call(
         kernel,
         out_shape=(field, field),
-        in_specs=[vmem, vmem, vmem, smem, smem, smem],
+        in_specs=[hbm] * 6,
         out_specs=(vmem, vmem),
-        scratch_shapes=[padded] * 8
-        + [lines] * 4
+        scratch_shapes=[padded, whole, whole]
+        + [pltpu.SMEM((LV - 1,), F32), pltpu.SMEM((LV,), F32), pltpu.SMEM((LV,), F32)]
+        + [padded] * 10
+        + [lines] * 6
         + [rims, rims, corners, corners, rims, rims, corners, corners]
         + [
             pltpu.VMEM((3, DIMS[1] * NG, 128), F32),
@@ -669,10 +775,13 @@
             pltpu.VMEM((NG, GP, NT), F32),
             pltpu.VMEM((NT - 1, 1, LP * PX), F32),
             pltpu.VMEM((DIMS[1] * NG, 1, 128), F32),
-            dma((2,)),
-            dma((2,)),
-            dma((2, 4)),
-            dma((2, 4)),
+            pltpu.VMEM((LV, CY), F32),
+            pltpu.VMEM((LV, CY), F32),
+            dma((6,)),
+            dma((3,)),
+            dma((3,)),
+            dma((3, 4)),
+            dma((3, 4)),
             dma((3,)),
             dma((3,)),
             dma((3,)),

time: 114 us -> 99.8 us (0.88)
  Pallas kernels: 106 us -> 92.6 us
    pallas_call x1, Pallas kernels: 106 us -> 92.6 us  [per_device(): pl.pallas_call(kernel, out_shape=(field, field), in_specs=[hbm] * 6, out_...]
where the time goes in v2:
time: 99.8 us; the launch traced here: 99.5 us
  Pallas kernels  92.6 us (93%)
  local copies, waits for them, and re-layouts  6.26 us (6%)
    pallas_call x1, Pallas kernels, per_device(): pl.pallas_call(kernel, out_shape=(field, field), in_specs=[hbm] * 6, out_...  92.6 us
    unnamed x14, local copies, waits for them, and re-layouts  6.26 us

profile of v2, /device:TPU:1, one launch (start us, length us, event | category | flops | bytes accessed | tf_op | source)
XLA Modules:
  0.0 99.5 jit_solution(5583808439122159798)
XLA Ops:
  0.6 0.0 copy-start
  0.6 0.9 copy-done
  1.6 0.0 copy-start.1
  1.6 1.0 copy-done.1
  2.5 0.0 copy-start.2
  2.6 1.0 copy-done.2
  3.5 0.0 copy-start.3
  3.5 0.7 copy-done.3
  4.2 0.0 copy-start.4
  4.2 0.7 copy-done.4
  4.8 0.0 copy-start.5
  4.8 0.7 copy-done.5
  5.5 92.6 %step.1 = (f32[70,8,128]{2,1,0:T(8,128)S(1)}, f32[70,8,128]{2,1,0:T(8,128)S(1)}) custom-call(f32[70,8,128]{2,1,0:T(8,128)S(1)} %copy-done, f32[70,8,128]{2,1,0:T(8,128)S(1)} %copy-done.1, f32[70,8,128]{2,1,0:T(8,128)S(1)} %copy-done.2, f32[69]{0:T(128)S(1)} %copy-done.3, f32[70]{0:T(128)S(1)} %copy-done.4, f32[70]{0:T(128)S(1)} %copy-done.5), custom_call_target="tpu_custom_call" | custom-call | tf_op jit(solution)/shard_map/step/pallas_call | solution.py:760
  98.1 0.7 copy.10
  98.8 0.7 copy.11
Async XLA Ops:
  0.6 1.0 copy-start
  1.6 1.0 copy-start.1
  2.5 1.0 copy-start.2
  3.5 0.7 copy-start.3
  4.2 0.7 copy-start.4
  4.8 0.7 copy-start.5

commit v3 on v2

--- a/solution.py
+++ b/solution.py
@@ -788,7 +788,7 @@
             dma((3,)),
         ],
         compiler_params=pltpu.CompilerParams(
-            collective_id=0, has_side_effects=True, vmem_limit_bytes=32 << 20
+            collective_id=0, has_side_effects=True, vmem_limit_bytes=67043328
         ),
         name="step",
     )(fv, sh, kel, link, longwave, shortwave)

time: 99.8 us -> 96.8 us (0.970)
  local copies, waits for them, and re-layouts: 6.26 us -> 2.45 us
  Pallas kernels: 92.6 us -> 93.6 us
    unnamed x14 -> x4, local copies, waits for them, and re-layouts: 6.26 us -> 2.45 us
where the time goes in v3:
time: 96.8 us; the launch traced here: 96.7 us
  Pallas kernels  93.6 us (97%)
  local copies, waits for them, and re-layouts  2.45 us (3%)
    pallas_call x1, Pallas kernels, per_device(): pl.pallas_call(kernel, out_shape=(field, field), in_specs=[hbm] * 6, out_...  93.6 us
    unnamed x4, local copies, waits for them, and re-layouts  2.45 us

profile of v3, /device:TPU:1, one launch (start us, length us, event | category | flops | bytes accessed | tf_op | source)
XLA Modules:
  0.0 96.7 jit_solution(88537912557237996)
XLA Ops:
  0.6 93.6 %step.1 = (f32[70,8,128]{2,1,0:T(8,128)}, f32[70,8,128]{2,1,0:T(8,128)}) custom-call(f32[70,8,128]{2,1,0:T(8,128)} %fv_hbm.1, f32[70,8,128]{2,1,0:T(8,128)} %sh_hbm.1, f32[70,8,128]{2,1,0:T(8,128)} %kel_hbm.1, f32[69]{0:T(128)} %link_hbm.1, f32[70]{0:T(128)} %longwave_hbm.1, f32[70]{0:T(128)} %shortwave_hbm.1), custom_call_target="tpu_custom_call" | custom-call | tf_op jit(solution)/shard_map/step/pallas_call | solution.py:760
  94.2 0.0 copy-start
  94.2 1.7 %copy.10 = f32[70,8,128]{2,1,0:T(8,128)} copy(f32[70,8,128]{2,1,0:T(8,128)} %get-tuple-element.4) | data formatting | bytes 573440
  96.0 0.0 copy-done
  96.0 0.7 copy.11
Async XLA Ops:
  94.2 1.7 %copy-start = (f32[70,8,128]{2,1,0:T(8,128)S(1)}, f32[70,8,128]{2,1,0:T(8,128)}, u32[]{:S(2)}) copy-start(f32[70,8,128]{2,1,0:T(8,128)} %get-tuple-element.5) | copy-start | bytes 860164

commit v4 on v3

--- a/solution.py
+++ b/solution.py
@@ -100,6 +100,7 @@
     shift_solve,
     image_solve,
     hs,
+    mid,
     hr,
     fs,
     fr,
@@ -122,6 +123,10 @@
     row_count,
     ghost_west,
     ghost_east,
+    turn_send_sem,
+    turn_recv_sem,
+    turn_own_sem,
+    own_sem,
     in_sem,
     a2a_send_sem,
     a2a_recv_sem,
@@ -171,6 +176,13 @@
 
         lax.fori_loop(max(low, 1), high, some, 0)
 
+    def each_plane(act):
+        def one(r, _):
+            act(r)
+            return 0
+
+        lax.fori_loop(1, np_, one, 0)
+
     plane_here = plane_base(0)
 
     def each_z(first, act):
@@ -191,8 +203,12 @@
     def greet(tile, grp):
         pl.semaphore_signal(barrier, inc=1, device_id=(tile, grp), device_id_type=MESH)
 
-    each_z(1, greet)
-    each_tile(0, np_, lambda tile: greet(tile, g))
+    ring_before = lax.rem(t + NT - 1, NT)
+    ring_after = lax.rem(t + 1, NT)
+    each_z(0, greet)
+    each_plane(lambda r: greet(plane_base(r) + z_part[0], g))
+    greet(ring_before, g)
+    greet(ring_after, g)
     pairs = (
         (kel_hbm, kel),
         (longwave_hbm, longwave),
@@ -217,8 +233,8 @@
     def a2a_start(src, dst, which, low, high):
         def send(peer):
             pltpu.make_async_remote_copy(
-                src_ref=src.at[pl.ds(peer, 1), :],
-                dst_ref=dst.at[pl.ds(t, 1), :],
+                src_ref=src.at[pl.ds(peer, 1)],
+                dst_ref=dst.at[pl.ds(t, 1)],
                 send_sem=a2a_send_sem.at[which],
                 recv_sem=a2a_recv_sem.at[which],
                 device_id=(peer, g),
@@ -226,6 +242,59 @@
             ).start()
 
         each_tile(low, high, send)
+
+    nxc = nx * nc
+    xc = lax.rem(t, nxc)
+
+    def turn_rows(dy):
+        return lax.rem(y + dy, ny)
+
+    def turn_start():
+        for dy in range(ny):
+            y2 = turn_rows(dy)
+            for dz in z_order[:-1]:
+                peer = plane_here + z_part[dz]
+                zh2 = lax.rem(zh + dz, nzh)
+                pltpu.make_async_remote_copy(
+                    src_ref=hs.at[pl.ds((y2 * nzh + zh2) * nxc, nxc)],
+                    dst_ref=mid.at[zh, pl.ds(y2 * nxc, nxc)],
+                    send_sem=turn_send_sem,
+                    recv_sem=turn_recv_sem.at[dy],
+                    device_id=(peer, g),
+                    device_id_type=MESH,
+                ).start()
+            pltpu.make_async_copy(
+                hs.at[pl.ds((y2 * nzh + zh) * nxc, nxc)],
+                mid.at[zh, pl.ds(y2 * nxc, nxc)],
+                turn_own_sem.at[dy],
+            ).start()
+
+    def line_wait(count, sem):
+        part = line_count.at[pl.ds(0, count)]
+        pltpu.make_async_copy(part, part, sem).wait()
+
+    def turn_middle():
+        for dy in range(ny):
+            y2 = turn_rows(dy)
+            line_wait((nzh - 1) * nxc, turn_recv_sem.at[dy])
+            line_wait(nxc, turn_own_sem.at[dy])
+
+            def one(r, _, y2=y2):
+                xc2 = lax.rem(xc + r, nxc)
+                pltpu.make_async_remote_copy(
+                    src_ref=mid.at[:, y2 * nxc + xc2],
+                    dst_ref=hr.at[y, :, xc],
+                    send_sem=a2a_send_sem.at[0],
+                    recv_sem=a2a_recv_sem.at[0],
+                    device_id=((y2 * nzh + zh) * nxc + xc2, g),
+                    device_id_type=MESH,
+                ).start()
+                return 0
+
+            lax.fori_loop(1 if dy == 0 else 0, nxc, one, 0)
+        own_copy = pltpu.make_async_copy(mid.at[:, p], hr.at[y, :, xc], own_sem)
+        own_copy.start()
+        own_copy.wait()
 
     def a2a_wait(which):
         wait_lines(a2a_recv_sem.at[which])
@@ -356,17 +425,17 @@
         lv = slice(ch * 16, (ch + 1) * 16)
         heat = down[lv] + upw[lv] - mean[None]
         down[lv] = heat
-        hs[:, ch * 128 : (ch + 1) * 128] = heat.reshape(16 * PX, CY).T
+        hs[:, 0, ch * 128 : (ch + 1) * 128] = heat.reshape(16 * PX, CY).T
 
     def lines_of(field, dst):
         for ch in range(NCH):
-            dst[:, ch * 128 : (ch + 1) * 128] = (
+            dst[:, 0, ch * 128 : (ch + 1) * 128] = (
                 field[ch * 16 : (ch + 1) * 16].reshape(16 * PX, CY).T
             )
 
     def columns_of(src, ch):
         top = min(LV, (ch + 1) * 16)
-        block = src[:, ch * 128 : (ch + 1) * 128].T.reshape(16, PX, CY)
+        block = src[:, 0, ch * 128 : (ch + 1) * 128].T.reshape(16, PX, CY)
         return slice(ch * 16, top), block[: top - ch * 16]
 
     lines_of(fv, fs)
@@ -470,12 +539,12 @@
     shift_rims = column_solve(lambda k: sh[k], shift_solve)
     halo_fill(2, shift_solve, shift_rims)
 
-    pl.semaphore_wait(barrier, NT - 1 + (NG - 1) * nzh)
+    pl.semaphore_wait(barrier, nz - 1 + np_ - 1 + 2)
 
     gather_start(0, shift_row)
-    a2a_start(hs, hr, 0, 0, np_)
-    hr[pl.ds(t, 1), :] = hs[pl.ds(t, 1), :]
-    fr[pl.ds(t, 1), :] = fs[pl.ds(t, 1), :]
+    turn_start()
+    fr[pl.ds(t, 1)] = fs[pl.ds(t, 1)]
+    turn_middle()
     halos2 = halo_start(2)
     gather_middle(0)
 
@@ -591,9 +660,12 @@
         north = jnp.where(outer_n, v, north)
         return r - ((west + east) + (south + north)) + sh[k] * v
 
-    a2a_wait(0)
+    line_wait((np_ - 1) * nzh, a2a_recv_sem.at[0])
     for ch in range(NCH):
-        lv, block = columns_of(hr, ch)
+        top = min(LV, (ch + 1) * 16)
+        lv = slice(ch * 16, top)
+        block = hr[:, :, :, 0, ch * 128 : (ch + 1) * 128].reshape(NT, 128)
+        block = block.T.reshape(16, PX, CY)[: top - ch * 16]
         res[lv] = fv[lv] + block
 
     half = np_ // 2
@@ -700,7 +772,7 @@
     gather_start(2, pack_row([r_sum - q_sum, rq, rs, qq, qs] + edges(r_sum) + edges(q_sum) + [iq]))
     lines_of(smooth1, xs)
     a2a_start(xs, xr, 2, 0, half)
-    xr[pl.ds(t, 1), :] = xs[pl.ds(t, 1), :]
+    xr[pl.ds(t, 1)] = xs[pl.ds(t, 1)]
 
     a2a_wait(1)
     for ch in range(NCH):
@@ -738,8 +810,11 @@
         lv, block = columns_of(xr, ch)
         out_rad[lv] = scale0 * upw[lv] + step1 * block + by_tile[None]
 
+    line_wait((np_ - 1) * nzh, a2a_send_sem.at[0])
+    line_wait((nzh - 1) * np_, turn_send_sem)
     for which in range(3):
-        a2a_drain(which)
+        if which > 0:
+            a2a_drain(which)
         gather_drain(which)
     for copy in halos0 + halos1 + halos2:
         copy.wait_send()
@@ -753,7 +828,9 @@
     steps = int(math.log2(NT))
     padded = pltpu.VMEM((LP, PX, CY), F32)
     whole = pltpu.VMEM((LV, PX, CY), F32)
-    lines = pltpu.VMEM((NT, LP * PX), F32)
+    lines = pltpu.VMEM((NT, 1, LP * PX), F32)
+    middle = pltpu.VMEM((DIMS[1], np_, 1, LP * PX), F32)
+    turned = pltpu.VMEM((DIMS[0], DIMS[1], DIMS[2] * DIMS[3], 1, LP * PX), F32)
     rims = pltpu.VMEM((3, LV, CY), F32)
     corners = pltpu.VMEM((3, PX, CY), F32)
     dma = pltpu.SemaphoreType.DMA
@@ -765,7 +842,8 @@
         scratch_shapes=[padded, whole, whole]
         + [pltpu.SMEM((LV - 1,), F32), pltpu.SMEM((LV,), F32), pltpu.SMEM((LV,), F32)]
         + [padded] * 10
-        + [lines] * 6
+        + [lines, middle, turned]
+        + [lines] * 4
         + [rims, rims, corners, corners, rims, rims, corners, corners]
         + [
             pltpu.VMEM((3, DIMS[1] * NG, 128), F32),
@@ -777,6 +855,10 @@
             pltpu.VMEM((DIMS[1] * NG, 1, 128), F32),
             pltpu.VMEM((LV, CY), F32),
             pltpu.VMEM((LV, CY), F32),
+            dma,
+            dma((DIMS[0],)),
+            dma((DIMS[0],)),
+            dma,
             dma((6,)),
             dma((3,)),
             dma((3,)),

time: 96.8 us -> 95.2 us (0.983)
  Pallas kernels: 93.6 us -> 91.9 us
    pallas_call x1, Pallas kernels: 93.6 us -> 91.9 us  [per_device(): pl.pallas_call(kernel, out_shape=(field, field), in_specs=[hbm] * 6, out_...]
where the time goes in v4:
time: 95.2 us; the launch traced here: 95 us
  Pallas kernels  91.9 us (97%)
  local copies, waits for them, and re-layouts  2.45 us (3%)
    pallas_call x1, Pallas kernels, per_device(): pl.pallas_call(kernel, out_shape=(field, field), in_specs=[hbm] * 6, out_...  91.9 us
    unnamed x4, local copies, waits for them, and re-layouts  2.45 us

profile of v4, /device:TPU:1, one launch (start us, length us, event | category | flops | bytes accessed | tf_op | source)
XLA Modules:
  0.0 95.0 jit_solution(16894654317753429597)
XLA Ops:
  0.6 91.9 %step.1 = (f32[70,8,128]{2,1,0:T(8,128)}, f32[70,8,128]{2,1,0:T(8,128)}) custom-call(f32[70,8,128]{2,1,0:T(8,128)} %fv_hbm.1, f32[70,8,128]{2,1,0:T(8,128)} %sh_hbm.1, f32[70,8,128]{2,1,0:T(8,128)} %kel_hbm.1, f32[69]{0:T(128)} %link_hbm.1, f32[70]{0:T(128)} %longwave_hbm.1, f32[70]{0:T(128)} %shortwave_hbm.1), custom_call_target="tpu_custom_call" | custom-call | tf_op jit(solution)/shard_map/step/pallas_call | solution.py:837
  92.6 0.0 copy-start
  92.6 1.7 %copy.10 = f32[70,8,128]{2,1,0:T(8,128)} copy(f32[70,8,128]{2,1,0:T(8,128)} %get-tuple-element.4) | data formatting | bytes 573440
  94.3 0.0 copy-done
  94.3 0.7 copy.11
Async XLA Ops:
  92.6 1.7 %copy-start = (f32[70,8,128]{2,1,0:T(8,128)S(1)}, f32[70,8,128]{2,1,0:T(8,128)}, u32[]{:S(2)}) copy-start(f32[70,8,128]{2,1,0:T(8,128)} %get-tuple-element.5) | copy-start | bytes 860164

commit v5 on v4

--- a/solution.py
+++ b/solution.py
@@ -771,17 +771,16 @@
     r_sum, q_sum, rq, rs, qq, qs, iq = blocked(LV, moments1, (zeros,) * 7)
     gather_start(2, pack_row([r_sum - q_sum, rq, rs, qq, qs] + edges(r_sum) + edges(q_sum) + [iq]))
     lines_of(smooth1, xs)
-    a2a_start(xs, xr, 2, 0, half)
+    a2a_start(xs, xr, 2, 0, np_)
     xr[pl.ds(t, 1)] = xs[pl.ds(t, 1)]
 
+    gather_middle(2)
     a2a_wait(1)
     for ch in range(NCH):
         lv, block = columns_of(fr, ch)
         down[lv] = down[lv] + block
     plain_solve(down, upw)
 
-    gather_middle(2)
-    a2a_start(xs, xr, 2, half, np_)
     got = gather_end(2, 14)
     e1 = coarse_solve(got[0])
     w1 = differences(e1)

time: 95.2 us -> 95.8 us (level)
  no operation moved by 1% of the time
where the time goes in v5:
time: 95.8 us; the launch traced here: 95.6 us
  Pallas kernels  92.5 us (97%)
  local copies, waits for them, and re-layouts  2.45 us (3%)
    pallas_call x1, Pallas kernels, per_device(): pl.pallas_call(kernel, out_shape=(field, field), in_specs=[hbm] * 6, out_...  92.5 us
    unnamed x4, local copies, waits for them, and re-layouts  2.45 us

profile of v5, /device:TPU:1, one launch (start us, length us, event | category | flops | bytes accessed | tf_op | source)
XLA Modules:
  0.0 95.6 jit_solution(2312732857413101144)
XLA Ops:
  0.6 92.5 %step.1 = (f32[70,8,128]{2,1,0:T(8,128)}, f32[70,8,128]{2,1,0:T(8,128)}) custom-call(f32[70,8,128]{2,1,0:T(8,128)} %fv_hbm.1, f32[70,8,128]{2,1,0:T(8,128)} %sh_hbm.1, f32[70,8,128]{2,1,0:T(8,128)} %kel_hbm.1, f32[69]{0:T(128)} %link_hbm.1, f32[70]{0:T(128)} %longwave_hbm.1, f32[70]{0:T(128)} %shortwave_hbm.1), custom_call_target="tpu_custom_call" | custom-call | tf_op jit(solution)/shard_map/step/pallas_call | solution.py:836
  93.2 0.0 copy-start
  93.2 1.7 %copy.10 = f32[70,8,128]{2,1,0:T(8,128)} copy(f32[70,8,128]{2,1,0:T(8,128)} %get-tuple-element.4) | data formatting | bytes 573440
  94.9 0.0 copy-done
  94.9 0.7 copy.11
Async XLA Ops:
  93.2 1.7 %copy-start = (f32[70,8,128]{2,1,0:T(8,128)S(1)}, f32[70,8,128]{2,1,0:T(8,128)}, u32[]{:S(2)}) copy-start(f32[70,8,128]{2,1,0:T(8,128)} %get-tuple-element.5) | copy-start | bytes 860164
